TPU v7x, 128 devices: a whole 4x4x4 slice. The times are simulated.
128 devices in a mesh: query: 4 (over y), cluster: 32 (over x, z, core).
Axes of the slice: x: 4, y: 4, z: 4, core: 2. Of those that a mesh axis runs over, the one named last changes fastest.
Arguments:
- queries: bfloat16 [4, 4096, 768], P('query', 'cluster'), may hold values from -6 to 6
- positives: int32 [4, 4096], P('query'), may hold values from 0 to 131071, as said below
- neg_clusters: int32 [4, 1024], P('query', 'cluster'), may hold values from 0 to 2047, as said below
- owner_map: int32 [2048], replicated, may hold values from 0 to 2047, as said below
- label_codes: bfloat16 [2048, 64, 768], P('cluster', 'query'), may hold values from -1 to 1
- label_scales: float32 [2048, 64, 6], P('cluster', 'query'), may hold values from 0.5 to 5
- label_master: float32 [2048, 64, 768], P('cluster', 'query'), may hold values from -13.2 to 13.2
- first_moment: float32 [2048, 64, 768], P('cluster', 'query'), may hold values from -1.8 to 1.8
- second_moment: float32 [2048, 64, 768], P('cluster', 'query'), may hold values from 0.05 to 1
Outputs:
- query_grad: float32 [4, 4096, 768], P('query', 'cluster')
- new_codes: bfloat16 [2048, 64, 768], P('cluster', 'query')
- new_scales: float32 [2048, 64, 6], P('cluster', 'query')
- new_master: float32 [2048, 64, 768], P('cluster', 'query')
- new_first: float32 [2048, 64, 768], P('cluster', 'query')
- new_second: float32 [2048, 64, 768], P('cluster', 'query')
Inputs may be any that keep to these rules, and one draw needn't show every extreme that they name: `neg_clusters`: slots k * 32 to (k + 1) * 32 - 1 of a group are scored on index k of cluster. Among the slots of one such block, at most 2 name clusters whose owner_map value lies in one owner column (owner_map // 64), and every block has columns with exactly 2. All slots of one group name different clusters. `owner_map`: A permutation of the cluster ids. `positives`: each is c * 64 + r for a cluster c listed for the query's group and a row r.
All inputs are finite; a program needn't handle non-finite values. Where the computation divides by a largest or mean magnitude, that divisor is 1e-20 or more.
Results may differ from a plain program's by a relative error of at most 0.011.
Values may be sent and summed in bfloat16 or wider, within the bound.
No kernel may reach another device: no remote copies, remote signals or barrier semaphores. Data moves between devices by JAX's collectives and lax.ppermute only.
A program may use at most 128 MiB of HBM per device.

v0:
```python
import math

import jax
import jax.numpy as jnp
from jax import lax
from jax.experimental import pallas as pl
from jax.experimental.pallas import tpu as pltpu
from jax.sharding import PartitionSpec as P


BLK = 128

pos_weight = 64.0
beta_first = 0.9
beta_second = 0.95
learn_rate = 0.05
adam_eps = 1e-08
adam_step = 20.0
scale_eps = 1e-06

STEP = 4
SUB = 512
ID_ROWS = 16
SPLIT1, SPLIT2, SPLIT3 = 1,1,1

F32, BF16, I32 = jnp.float32, jnp.bfloat16, jnp.int32
ANY = pl.BlockSpec(memory_space=pl.ANY)
VMEM_LIMIT = 62 * 1024 * 1024


def dequant_kernel(codes_ref, scales_ref, rows_ref):
    rows, width = codes_ref.shape
    for blk in range(width // BLK):
        cols = slice(blk * BLK, (blk + 1) * BLK)
        scale = jnp.broadcast_to(scales_ref[:, blk : blk + 1], (rows, BLK))
        rows_ref[:, cols] = (codes_ref[:, cols].astype(F32) * scale).astype(BF16)


def dequantize(codes, scales):
    rows, width = codes.shape
    tile = min(256, rows)
    return pl.pallas_call(
        dequant_kernel,
        out_shape=jax.ShapeDtypeStruct((rows, width), BF16),
        grid=(rows // tile,),
        in_specs=[
            pl.BlockSpec((tile, width), lambda i: (i, 0)),
            pl.BlockSpec((tile, scales.shape[1]), lambda i: (i, 0)),
        ],
        out_specs=pl.BlockSpec((tile, width), lambda i: (i, 0)),
        name="dequantize",
        cost_estimate=pl.CostEstimate(
            flops=rows * width, bytes_accessed=4 * rows * width, transcendentals=0
        ),
    )(codes, scales)


def score_kernel(
    order_ref, base_ref, info_ref, pid_hbm, own_hbm, right_hbm, left_hbm, low_hbm, high_hbm, *refs
):
    q_pieces, refs = (refs[:5], refs[5:10]), refs[10:]
    mine_u, mine_v, part_u, part_v, lab_own, lab_a, lab_b, lab_c, lab_d = refs[:9]
    q_ref, qt_ref, ids_ref, pid_ref, w_ref, acc_ref, wb_ref, id_ref, sa_ref, sb_ref = refs[9:19]
    pa_ref, pb_ref, lt_ref, lab_ref, qg_ref, sem, q_sem, lab_sem, out_sem = refs[19:]
    total, width = q_ref.shape
    n_col, quarter = w_ref.shape[0] // 4, w_ref.shape[1]
    half = n_col // 2
    crows = 4 * quarter
    rows = STEP * crows
    n_pair = total // (2 * SUB)
    inv_root = 1.0 / math.sqrt(width)
    power_scale = math.log2(math.e) * inv_root
    listed = info_ref[0]
    my_y = info_ref[1]
    n_block = lax.div(listed + STEP - 1, STEP)

    def rows_of(start, size):
        return pl.ds(pl.multiple_of(start, size), size)

    my_col = info_ref[2]
    my_x, my_z, my_core = lax.div(my_col, 8), lax.rem(lax.div(my_col, 2), 4), lax.rem(my_col, 2)
    share = total // 32

    load_q = []
    for core in range(2):
        own_q, right_q, left_q, low_q, high_q = q_pieces[core]
        for z, x in ((z, x) for z in range(4) for x in range(4)):
            src = (own_q, right_q, (low_q, high_q)[x // 2], left_q)[z].at[x % 2 if z == 2 else x]
            col = (lax.rem(my_x + x, 4) * 4 + lax.rem(my_z + z, 4)) * 2
            col = col + (my_core if core == 0 else 1 - my_core)
            load_q.append(
                pltpu.make_async_copy(
                    src.at[pl.ds(0, share)], q_ref.at[rows_of(col * share, share)], q_sem.at[col]
                )
            )
    targets = ((0, n_col), (n_col, n_col), (3 * n_col, n_col), (2 * n_col, half), (2 * n_col + half, half))
    pieces = (own_hbm, right_hbm, left_hbm, low_hbm, high_hbm)
    loads = [
        pltpu.make_async_copy(src, w_ref.at[pl.ds(*at)], sem.at[i])
        for i, (src, at) in enumerate(zip(pieces, targets, strict=True))
    ]
    load_ids = pltpu.make_async_copy(pid_hbm, ids_ref, sem.at[5])
    load_ids.start()
    for copy in load_q + loads:
        copy.start()

    def clear(entry, carry):
        where = order_ref[entry]
        for j in range(4):
            lab_ref[j * n_col + where] = jnp.zeros((quarter, width), BF16)
        return carry

    lax.fori_loop(listed, n_col, clear, 0)

    load_ids.wait()

    def spread(i, carry):
        row = jnp.broadcast_to(ids_ref[pl.ds(i, 1), :], (128, 128))
        pid_ref[rows_of(i * 128, 128), :] = row.T
        return carry

    lax.fori_loop(0, total // 128, spread, 0)

    def flip(i, carry):
        for h in range(2):
            k = 2 * i + h
            pltpu.make_async_copy(
                q_pieces[0][0].at[0, pl.ds(0, share)], q_ref.at[rows_of(k * share, share)], q_sem.at[k]
            ).wait()
        at = rows_of(i * 2 * share, 2 * share)
        qt_ref[:, at] = q_ref[at, :].T
        return carry

    lax.fori_loop(0, 16, flip, 0)

    for copy in loads:
        copy.wait()

    lane = lax.broadcasted_iota(I32, (8, rows), 1)
    slot = lax.div(lane, jnp.full_like(lane, crows))
    within = lax.rem(lane, jnp.full_like(lane, crows))
    part = lax.rem(lax.div(within, jnp.full_like(lane, quarter)) + my_y, jnp.full_like(lane, 4))
    row_id = part * quarter + lax.rem(within, jnp.full_like(lane, quarter))

    def stage(block):
        buf = lax.rem(block, 2)
        ids = row_id
        for k in range(STEP):
            entry = jnp.minimum(block * STEP + k, n_col - 1)
            valid = block * STEP + k < listed
            where = order_ref[entry]
            ids = ids + jnp.where(slot == k, base_ref[entry], 0)
            for j in range(4):
                start = k * crows + j * quarter
                held = w_ref[j * n_col + where]
                wb_ref[buf, start : start + quarter, :] = jnp.where(
                    valid, held, jnp.zeros_like(held)
                )
        id_ref[buf] = ids

    def score(block, start, to_ref):
        size = SUB // SPLIT1
        for h in range(SPLIT1):
            to_ref[h * size : (h + 1) * size] = lax.dot_general(
                q_ref[rows_of(start + h * size, size), :],
                wb_ref[lax.rem(block, 2)],
                (((1,), (1,)), ((), ())),
                preferred_element_type=F32,
            )

    def slopes(block, start, from_ref, to_ref):
        pid = pid_ref[rows_of(start, SUB), :]
        ids = id_ref[lax.rem(block, 2)]
        for c in range(rows // 128):
            cols = slice(c * 128, (c + 1) * 128)
            hit = pid == ids[0:1, cols]
            power = from_ref[:, cols] * jnp.where(hit, power_scale, -power_scale)
            prob = jnp.where(hit, -pos_weight, 1.0) / (1.0 + jnp.exp2(power))
            to_ref[:, cols] = prob.astype(BF16)

    def grads(block, start, p_ref, lt_is_new):
        size = SUB // SPLIT2
        for h in range(SPLIT2):
            at = rows_of(start + h * size, size)
            old = jnp.where(block == 0, 0.0, acc_ref[at, :])
            acc_ref[at, :] = old + jnp.dot(
                p_ref[h * size : (h + 1) * size],
                wb_ref[lax.rem(block, 2)],
                preferred_element_type=F32,
            )
        buf = lax.rem(block, 2)
        size = width // SPLIT3
        for h in range(SPLIT3):
            cols = slice(h * size, (h + 1) * size)
            old = jnp.where(lt_is_new, 0.0, lt_ref[buf, cols])
            lt_ref[buf, cols] = old + jnp.dot(
                qt_ref[cols, rows_of(start, SUB)], p_ref[...], preferred_element_type=F32
            )

    def emit(block):
        lab = (lt_ref[lax.rem(block, 2)] * inv_root).T
        for k in range(STEP):
            entry = block * STEP + k

            @pl.when(entry < listed)
            def _(k=k, entry=entry):
                where = order_ref[entry]
                for j in range(4):
                    start = k * crows + j * quarter
                    lab_ref[j * n_col + where] = lab[start : start + quarter, :].astype(BF16)

    @pl.when(n_block > 0)
    def _():
        stage(0)
        score(0, 0, sa_ref)
        pb_ref[...] = jnp.zeros_like(pb_ref)

    def pair(t, carry):
        block, at = lax.div(t, n_pair), lax.rem(t, n_pair)
        before = jnp.maximum(t - 1, 0)
        pblock, pat = lax.div(before, n_pair), lax.rem(before, n_pair)
        nblock, nat = lax.div(t + 1, n_pair), lax.rem(t + 1, n_pair)
        here = at * (2 * SUB)

        @pl.when(nat == 0)
        def _():
            stage(nblock)

        @pl.when((at == 1) & (block > 0))
        def _():
            emit(block - 1)

        slopes(block, here, sa_ref, pa_ref)
        score(block, here + SUB, sb_ref)
        grads(pblock, pat * (2 * SUB) + SUB, pb_ref, False)
        slopes(block, here + SUB, sb_ref, pb_ref)
        score(nblock, nat * (2 * SUB), sa_ref)
        grads(block, here, pa_ref, at == 0)
        return carry

    lax.fori_loop(0, n_block * n_pair, pair, 0)

    @pl.when(n_block > 0)
    def _():
        grads(n_block - 1, total - SUB, pb_ref, False)
        emit(n_block - 1)

    put_lab = []
    at = 0
    for i, out in enumerate((lab_own, lab_a, lab_b, lab_c, lab_d)):
        size = out.shape[0]
        put_lab.append(pltpu.make_async_copy(lab_ref.at[pl.ds(at, size)], out, lab_sem.at[i]))
        put_lab[-1].start()
        at += size

    part_rows = share // 2

    def puts(k, out_u, out_v):
        x, z = lax.rem(lax.div(k, 8) + 4 - my_x, 4), lax.rem(lax.div(k, 2) + 8 - my_z, 4)
        return (
            pltpu.make_async_copy(
                qg_ref.at[rows_of(k * share, part_rows)], out_u.at[x * 4 + z], out_sem.at[0, k]
            ),
            pltpu.make_async_copy(
                qg_ref.at[rows_of(k * share + part_rows, part_rows)],
                out_v.at[z * 4 + x],
                out_sem.at[1, k],
            ),
        )

    def finish(k, carry):
        at = rows_of(k * share, share)
        qg_ref[at, :] = jnp.where(n_block > 0, acc_ref[at, :] * inv_root, 0.0).astype(BF16)

        @pl.when(lax.rem(k, 2) == my_core)
        def _():
            for copy in puts(k, mine_u, mine_v):
                copy.start()

        @pl.when(lax.rem(k, 2) != my_core)
        def _():
            for copy in puts(k, part_u, part_v):
                copy.start()

        return carry

    lax.fori_loop(0, 32, finish, 0)

    def settle(k, carry):
        for copy in puts(k, mine_u, mine_v):
            copy.wait()
        return carry

    lax.fori_loop(0, 32, settle, 0)
    for copy in put_lab:
        copy.wait()


def score_and_grads(order, base, info, pid, quarters, queries):
    total, width = pid.size, quarters[0].shape[2]
    n_col, quarter = quarters[0].shape[0], quarters[0].shape[1]
    half = n_col // 2
    block = STEP * 4 * quarter
    smem = pl.BlockSpec(memory_space=pltpu.SMEM)
    share = jax.ShapeDtypeStruct((16, total // 64, width), BF16)
    label = lambda size: jax.ShapeDtypeStruct((size, quarter, width), BF16)
    return pl.pallas_call(
        score_kernel,
        out_shape=(share,) * 4
        + (label(n_col), label(half), label(n_col), label(n_col), label(half)),
        in_specs=[smem] * 3 + [ANY] * 16,
        out_specs=(ANY,) * 9,
        scratch_shapes=[
            pltpu.VMEM((total, width), BF16),
            pltpu.VMEM((width, total), BF16),
            pltpu.VMEM((total // 128, 128), I32),
            pltpu.VMEM((total, 128), I32),
            pltpu.VMEM((4 * n_col, quarter, width), BF16),
            pltpu.VMEM((total, width), F32),
            pltpu.VMEM((2, block, width), BF16),
            pltpu.VMEM((2, 8, block), I32),
            pltpu.VMEM((SUB, block), F32),
            pltpu.VMEM((SUB, block), F32),
            pltpu.VMEM((SUB, block), BF16),
            pltpu.VMEM((SUB, block), BF16),
            pltpu.VMEM((2, width, block), F32),
            pltpu.VMEM((4 * n_col, quarter, width), BF16),
            pltpu.VMEM((total, width), BF16),
            pltpu.SemaphoreType.DMA((6,)),
            pltpu.SemaphoreType.DMA((32,)),
            pltpu.SemaphoreType.DMA((5,)),
            pltpu.SemaphoreType.DMA((2, 32)),
        ],
        compiler_params=pltpu.CompilerParams(vmem_limit_bytes=VMEM_LIMIT),
        name="score",
        cost_estimate=pl.CostEstimate(
            flops=3 * total * n_col * 2 * quarter * width * 2,
            bytes_accessed=4 * total * width + 16 * n_col * quarter * width,
            transcendentals=total * n_col * 4 * quarter,
        ),
    )(order, base, info, pid, *quarters, *queries)


def update_kernel(
    own_ref, left_ref, right_ref, master_ref, first_ref, second_ref,
    codes_ref, scales_ref, master_out, first_out, second_out,
):
    width = master_ref.shape[1]
    fix_first = 1.0 - beta_first**adam_step
    fix_second = 1.0 - beta_second**adam_step
    peaks = []
    for blk in range(width // BLK):
        cols = slice(blk * BLK, (blk + 1) * BLK)
        grad = (
            own_ref[:, cols].astype(F32)
            + left_ref[:, cols].astype(F32)
            + right_ref[:, cols].astype(F32)
        )
        first = beta_first * first_ref[:, cols] + (1.0 - beta_first) * grad
        second = beta_second * second_ref[:, cols] + (1.0 - beta_second) * grad * grad
        master = master_ref[:, cols] - learn_rate * (first / fix_first) / (
            jnp.sqrt(second / fix_second) + adam_eps
        )
        peak = jnp.max(jnp.abs(master), axis=1, keepdims=True) + scale_eps
        codes_ref[:, cols] = (master / peak).astype(BF16)
        master_out[:, cols] = master
        first_out[:, cols] = first
        second_out[:, cols] = second
        peaks.append(peak)
    scales_ref[...] = jnp.concatenate(peaks, axis=1)


def update(own, left, right, master, first, second):
    rows, width = master.shape
    tile = min(128, rows)
    spec = pl.BlockSpec((tile, width), lambda i: (i, 0))
    blocks = width // BLK
    return pl.pallas_call(
        update_kernel,
        out_shape=(
            jax.ShapeDtypeStruct((rows, width), BF16),
            jax.ShapeDtypeStruct((rows, blocks), F32),
            jax.ShapeDtypeStruct((rows, width), F32),
            jax.ShapeDtypeStruct((rows, width), F32),
            jax.ShapeDtypeStruct((rows, width), F32),
        ),
        grid=(rows // tile,),
        in_specs=[spec] * 6,
        out_specs=(spec, pl.BlockSpec((tile, blocks), lambda i: (i, 0)), spec, spec, spec),
        compiler_params=pltpu.CompilerParams(vmem_limit_bytes=32 * 1024 * 1024),
        name="update",
        cost_estimate=pl.CostEstimate(
            flops=20 * rows * width, bytes_accessed=32 * rows * width, transcendentals=rows * width
        ),
    )(own, left, right, master, first, second)


def shift(value, by):
    size = lax.axis_size("query")
    return lax.ppermute(value, "query", [(i, (i + by) % size) for i in range(size)])


def place(x, z, core):
    return (x % 4 * 4 + z % 4) * 2 + core


def hop(value, x=0, z=0, core=0):
    pairs = [
        (place(a, b, c), place(a + x, b + z, c ^ core))
        for a in range(4)
        for b in range(4)
        for c in range(2)
    ]
    return lax.ppermute(value, "cluster", pairs)


def add(*values):
    return sum(value.astype(F32) for value in values).astype(BF16)


def ring_open(b, c, send):
    return send(b, 1), send(c, -1)


def ring_close(own, a, d, left, right, send):
    half = a.shape[0]
    left_low = send(add(a, left[half:]), 1)
    right_high = send(add(d, right[:half]), -1)
    return (own, jnp.concatenate([left_low, left[:half]]), jnp.concatenate([right[half:], right_high]))


def ring_sum(value, send):
    own, a, b, c, d = cut(value)
    return add(*ring_close(own, a, d, *ring_open(b, c, send), send))


def cut(value):
    n = value.shape[0] // 4
    half = n // 2
    return value[:n], value[n : n + half], value[n + half : 2 * n + half], value[2 * n + half : 4 * n - half], value[4 * n - half :]


def ring_sum_small(value, send):
    n = value.shape[0] // 4
    parts = [send(value[j * n : (j + 1) * n], j if j < 3 else -1) for j in range(1, 4)]
    return add(value[:n], *parts)


def along_x(value, by):
    return hop(value, x=by)


def along_z(value, by):
    return hop(value, z=by)


def per_device(
    queries,
    positives,
    neg_clusters,
    owner_map,
    label_codes,
    label_scales,
    label_master,
    first_moment,
    second_moment,
):
    n_col, quarter, width = label_codes.shape
    crows = 4 * quarter
    half = n_col // 2
    my_y = lax.axis_index("query")
    my_col = lax.axis_index("cluster")

    own = dequantize(
        label_codes.reshape(n_col * quarter, width),
        label_scales.reshape(n_col * quarter, width // BLK),
    ).reshape(n_col, quarter, width)
    left, right = shift(own, 1), shift(own, -1)

    pair_ids = jnp.concatenate([neg_clusters, hop(neg_clusters, core=1)], axis=1)
    digits = jnp.concatenate([pair_ids // 64, pair_ids % 64], axis=1).astype(BF16)
    digits = jnp.pad(digits, ((0, ID_ROWS - 1), (0, width - digits.shape[1])))
    mine = jnp.concatenate([queries[0], digits])
    half_rows = mine.shape[0] // 2
    x_left, x_right = along_x(mine, 1), along_x(mine, -1)
    x_low, x_high = along_x(x_left[:half_rows], 1), along_x(x_right[half_rows:], -1)
    strip = jnp.stack([mine, x_right, jnp.concatenate([x_low, x_high]), x_left])
    z_left, z_right = along_z(strip, 1), along_z(strip, -1)
    far_low, far_high = shift(left[:half], 1), shift(right[half:], -1)
    z_low, z_high = along_z(z_left[:2], 1), along_z(z_right[2:], -1)
    pieces = (strip, z_right, z_left, z_low, z_high)
    pieces = pieces + (hop(strip, core=1),)
    pieces = pieces + (hop(z_right, core=1), hop(z_left, core=1))
    pieces = pieces + (hop(z_low, core=1), hop(z_high, core=1))
    digits = jnp.concatenate([piece[:, -ID_ROWS, :128] for piece in pieces[:5]]).astype(I32)
    group_ids = (digits[:, :64] * 64 + digits[:, 64:]).reshape(-1)

    places = my_col * n_col + jnp.arange(n_col, dtype=I32)
    all_ids = jnp.arange(owner_map.shape[0], dtype=I32)
    held = jnp.sum(jnp.where(owner_map[None, :] == places[:, None], all_ids[None, :], 0), axis=1)
    listed = jnp.sum((group_ids[None, :] == held[:, None]).astype(I32), axis=1)
    count = jnp.sum(listed)
    local = jnp.arange(n_col, dtype=I32)
    before = local[None, :] < local[:, None]
    ahead = jnp.sum(jnp.where(before, listed[None, :], 0), axis=1)
    rank = jnp.where(listed > 0, ahead, count + local - ahead)
    place = rank[None, :] == local[:, None]
    order = jnp.sum(jnp.where(place, local[None, :], 0), axis=1)
    base = jnp.sum(jnp.where(place, held[None, :], 0), axis=1) * crows
    info = jnp.stack([count, my_y.astype(I32), my_col.astype(I32)])
    *query_parts, label_own, label_a, label_b, label_c, label_d = score_and_grads(
        order,
        base,
        info,
        positives.reshape(-1, 128),
        (own, right, left, far_low, far_high),
        pieces,
    )
    label_hops = ring_open(label_b, label_c, shift)
    mine_u, mine_v, part_u, part_v = query_parts
    u = add(mine_u, hop(part_u, core=1))
    v = add(mine_v, hop(part_v, core=1))
    u = ring_sum(u, along_x)
    v = ring_sum(v, along_z)
    label_left, label_right, u, v = lax.optimization_barrier((*label_hops, u, v))
    label_parts = ring_close(label_own, label_a, label_d, label_left, label_right, shift)
    u = ring_sum_small(u, along_z)
    v = ring_sum_small(v, along_x)
    query_grad = jnp.concatenate([u[0], v[0]]).astype(F32)

    flat = lambda value: value.reshape(n_col * quarter, width)
    new_codes, new_scales, new_master, new_first, new_second = update(
        *(flat(part) for part in label_parts),
        flat(label_master),
        flat(first_moment),
        flat(second_moment),
    )
    shape = label_master.shape
    return (
        query_grad[None],
        new_codes.reshape(shape),
        new_scales.reshape(n_col, quarter, width // BLK),
        new_master.reshape(shape),
        new_first.reshape(shape),
        new_second.reshape(shape),
    )


def solution(mesh):
    in_specs = (
        P("query", "cluster", None),
        P("query", None),
        P("query", "cluster"),
        P(),
        P("cluster", "query", None),
        P("cluster", "query", None),
        P("cluster", "query", None),
        P("cluster", "query", None),
        P("cluster", "query", None),
    )
    out_specs = (
        P("query", "cluster", None),
        P("cluster", "query", None),
        P("cluster", "query", None),
        P("cluster", "query", None),
        P("cluster", "query", None),
        P("cluster", "query", None),
    )

    return jax.shard_map(
        per_device, mesh=mesh, in_specs=in_specs, out_specs=out_specs, check_vma=False
    )
```

profile of v0, /device:TPU:4, one launch (start us, length us, event | category | flops | bytes accessed | tf_op | source)
XLA Modules:
  0.0 242.8 jit_solution(2917876571486494487)
XLA Ops:
  5.9 5.5 %collective-permute-done.1 = bf16[144,768]{1,0:T(8,128)(2,1)S(1)} collective-permute-done((bf16[144,768]{1,0:T(8,128)(2,1)S(1)}, bf16[144,768]{1,0:T(8,128)(2,1)S(1)}, u32[]{:S(2)}, u32[]{:S(2)}) %collective-permute-start.1) | collective-permute-done | bytes 221216 | tf_op jit(solution)/shard_map/ppermute | solution.py:414
  12.0 2.0 collective-permute-start.3
  14.0 1.9 copy.34
  15.8 4.1 %dequantize.1 = bf16[1024,768]{1,0:T(8,128)(2,1)} custom-call(bf16[1024,768]{1,0:T(8,128)(2,1)} %bitcast.54, f32[1024,6]{1,0:T(8,128)} %bitcast.53), custom_call_target="tpu_custom_call" | custom-call | flops 786432 | bytes 3145728 | tf_op jit(solution)/shard_map/dequantize/pallas_call | solution.py:42
  23.4 2.0 collective-permute-start.6
  25.3 2.2 collective-permute-start.5
  27.6 18.4 %collective-permute-done.6.refs_2_ = bf16[4,144,768]{2,1,0:T(8,128)(2,1)} collective-permute-done((bf16[4,144,768]{2,1,0:T(8,128)(2,1)S(1)}, bf16[4,144,768]{2,1,0:T(8,128)(2,1)}, u32[]{:S(2)}, u32[]{:S(2)}) %collective-permute-start.6) | collective-permute-done | bytes 884768 | tf_op jit(solution)/shard_map/ppermute | solution.py:414
  45.9 1.8 slice.177
  48.8 3.3 %collective-permute-start.8 = (bf16[2,144,768]{2,1,0:T(8,128)(2,1)S(1)}, bf16[2,144,768]{2,1,0:T(8,128)(2,1)}, u32[]{:S(2)}, u32[]{:S(2)}) collective-permute-start(bf16[2,144,768]{2,1,0:T(8,128)(2,1)S(1)} %slice.179), channel_id=1, source_target_pairs={{0,6},{1,7},{2,0},{3,1},{4,2},{5,3},{6,4},{7,5},{8,14},{9,15},{10,... | collective-permute-start | bytes 1327112 | tf_op jit(solution)/shard_map/ppermute | solution.py:414
  53.7 3.1 %collective-permute-done.10.left_hbm = bf16[64,16,768]{2,1,0:T(8,128)(2,1)} collective-permute-done((bf16[64,16,768]{2,1,0:T(8,128)(2,1)}, bf16[64,16,768]{2,1,0:T(8,128)(2,1)}, u32[]{:S(2)}, u32[]{:S(2)}) %collective-permute-start.10) | collective-permute-done | bytes 1572896 | tf_op jit(solution)/shard_map/ppermute | solution.py:400
  62.6 2.9 %collective-permute-start.12 = (bf16[32,16,768]{2,1,0:T(8,128)(2,1)S(1)}, bf16[32,16,768]{2,1,0:T(8,128)(2,1)S(1)}, u32[]{:S(2)}, u32[]{:S(2)}) collective-permute-start(bf16[32,16,768]{2,1,0:T(8,128)(2,1)S(1)} %slice.184), channel_id=1, source_target_pairs={{0,96},{32,0},{64,32},{96,64},{1,97},{33,1},{65,33},{97,65},{2,98}... | collective-permute-start | bytes 2359304 | tf_op jit(solution)/shard_map/ppermute | solution.py:400
  69.1 11.7 %collective-permute-done.11.low_hbm = bf16[32,16,768]{2,1,0:T(8,128)(2,1)} collective-permute-done((bf16[32,16,768]{2,1,0:T(8,128)(2,1)S(1)}, bf16[32,16,768]{2,1,0:T(8,128)(2,1)}, u32[]{:S(2)}, u32[]{:S(2)}) %collective-permute-start.11) | collective-permute-done | bytes 786464 | tf_op jit(solution)/shard_map/ppermute | solution.py:400
  80.7 2.3 collective-permute-done.12.high_hbm
  83.9 58.7 %score.1 = (bf16[16,64,768]{2,1,0:T(8,128)(2,1)}, bf16[16,64,768]{2,1,0:T(8,128)(2,1)}, bf16[16,64,768]{2,1,0:T(8,128)(2,1)}, bf16[16,64,768]{2,1,0:T(8,128)(2,1...) custom-call(s32[64]{0:T(128)} %get-tuple-element.75.order_ref, ...), custom_call_target="tpu_custom_call" | custom-call | flops 38654705664 | bytes 25165824 | tf_op jit(solution)/shard_map/score/pallas_call | solution.py:307
  142.7 12.1 %collective-permute-start.20 = (bf16[16,64,768]{2,1,0:T(8,128)(2,1)}, bf16[16,64,768]{2,1,0:T(8,128)(2,1)S(1)}, u32[]{:S(2)}, u32[]{:S(2)}) collective-permute-start(bf16[16,64,768]{2,1,0:T(8,128)(2,1)} %get-tuple-element.27), channel_id=1, source_target_pairs={{0,1},{1,0},{2,3},{3,2},{4,5},{5,4},{6,7},{7,6},{8,9},{9,8},{10,11... | collective-permute-start | bytes 4718600 | tf_op jit(solution)/shard_map/ppermute | solution.py:414
  154.9 1.9 collective-permute-start.18
  156.8 1.8 collective-permute-start.19
  158.6 1.9 add_convert_fusion.1
  160.6 6.1 %collective-permute-start.23 = (bf16[4,64,768]{2,1,0:T(8,128)(2,1)S(1)}, bf16[4,64,768]{2,1,0:T(8,128)(2,1)S(1)}, u32[]{:S(2)}, u32[]{:S(2)}) collective-permute-start(bf16[4,64,768]{2,1,0:T(8,128)(2,1)S(1)} %get-tuple-element.84), channel_id=1, source_target_pairs={{0,24},{1,25},{2,26},{3,27},{4,28},{5,29},{6,30},{7,31},{8,0},{9,1... | collective-permute-start | bytes 1179656 | tf_op jit(solution)/shard_map/ppermute | solution.py:414
  167.9 7.5 %collective-permute-done.23 = bf16[4,64,768]{2,1,0:T(8,128)(2,1)S(1)} collective-permute-done((bf16[4,64,768]{2,1,0:T(8,128)(2,1)S(1)}, bf16[4,64,768]{2,1,0:T(8,128)(2,1)S(1)}, u32[]{:S(2)}, u32[]{:S(2)}) %collective-permute-start.23) | collective-permute-done | bytes 393248 | tf_op jit(solution)/shard_map/ppermute | solution.py:414
  175.3 5.0 %collective-permute-start.26 = (bf16[4,64,768]{2,1,0:T(8,128)(2,1)S(1)}, bf16[4,64,768]{2,1,0:T(8,128)(2,1)S(1)}, u32[]{:S(2)}, u32[]{:S(2)}) collective-permute-start(bf16[4,64,768]{2,1,0:T(8,128)(2,1)S(1)} %get-tuple-element.81), channel_id=1, source_target_pairs={{0,2},{1,3},{2,4},{3,5},{4,6},{5,7},{6,0},{7,1},{8,10},{9,11},{10,... | collective-permute-start | bytes 1179656 | tf_op jit(solution)/shard_map/ppermute | solution.py:414
  180.8 1.7 collective-permute-start.22
  182.6 5.3 %collective-permute-done.26 = bf16[4,64,768]{2,1,0:T(8,128)(2,1)S(1)} collective-permute-done((bf16[4,64,768]{2,1,0:T(8,128)(2,1)S(1)}, bf16[4,64,768]{2,1,0:T(8,128)(2,1)S(1)}, u32[]{:S(2)}, u32[]{:S(2)}) %collective-permute-start.26) | collective-permute-done | bytes 393248 | tf_op jit(solution)/shard_map/ppermute | solution.py:414
  188.0 3.2 %collective-permute-start.29 = (bf16[2,64,768]{2,1,0:T(8,128)(2,1)S(1)}, bf16[2,64,768]{2,1,0:T(8,128)(2,1)S(1)}, u32[]{:S(2)}, u32[]{:S(2)}) collective-permute-start(bf16[2,64,768]{2,1,0:T(8,128)(2,1)S(1)} %get-tuple-element.78), channel_id=1, source_target_pairs={{0,6},{1,7},{2,0},{3,1},{4,2},{5,3},{6,4},{7,5},{8,14},{9,15},{10,... | collective-permute-start | bytes 589832 | tf_op jit(solution)/shard_map/ppermute | solution.py:414
  191.6 2.8 %collective-permute-done.29 = bf16[2,64,768]{2,1,0:T(8,128)(2,1)S(1)} collective-permute-done((bf16[2,64,768]{2,1,0:T(8,128)(2,1)S(1)}, bf16[2,64,768]{2,1,0:T(8,128)(2,1)S(1)}, u32[]{:S(2)}, u32[]{:S(2)}) %collective-permute-start.29) | collective-permute-done | bytes 196640 | tf_op jit(solution)/shard_map/ppermute | solution.py:414
  194.4 3.9 %collective-permute-done.27 = bf16[2,64,768]{2,1,0:T(8,128)(2,1)S(1)} collective-permute-done((bf16[2,64,768]{2,1,0:T(8,128)(2,1)S(1)}, bf16[2,64,768]{2,1,0:T(8,128)(2,1)S(1)}, u32[]{:S(2)}, u32[]{:S(2)}) %collective-permute-start.27) | collective-permute-done | bytes 196640 | tf_op jit(solution)/shard_map/ppermute | solution.py:414
  198.4 12.4 %collective-permute-done.19 = bf16[64,16,768]{2,1,0:T(8,128)(2,1)S(1)} collective-permute-done((bf16[64,16,768]{2,1,0:T(8,128)(2,1)}, bf16[64,16,768]{2,1,0:T(8,128)(2,1)S(1)}, u32[]{:S(2)}, u32[]{:S(2)}) %collective-permute-start.19) | collective-permute-done | bytes 1572896 | tf_op jit(solution)/shard_map/ppermute | solution.py:400
  210.9 3.2 %collective-permute-start.32 = (bf16[1,64,768]{2,1,0:T(8,128)(2,1)S(1)}, bf16[1,64,768]{2,1,0:T(8,128)(2,1)S(1)}, u32[]{:S(2)}, u32[]{:S(2)}) collective-permute-start(bf16[1,64,768]{2,1,0:T(8,128)(2,1)S(1)} %get-tuple-element.87), channel_id=1, source_target_pairs={{0,6},{1,7},{2,0},{3,1},{4,2},{5,3},{6,4},{7,5},{8,14},{9,15},{10,... | collective-permute-start | bytes 294920 | tf_op jit(solution)/shard_map/ppermute | solution.py:414
  222.4 4.0 %collective-permute-done.34 = bf16[1,64,768]{2,1,0:T(8,128)(2,1)S(1)} collective-permute-done((bf16[1,64,768]{2,1,0:T(8,128)(2,1)S(1)}, bf16[1,64,768]{2,1,0:T(8,128)(2,1)S(1)}, u32[]{:S(2)}, u32[]{:S(2)}) %collective-permute-start.34) | collective-permute-done | bytes 98336 | tf_op jit(solution)/shard_map/ppermute | solution.py:414
  227.2 5.6 %collective-permute-done.37 = bf16[32,16,768]{2,1,0:T(8,128)(2,1)S(1)} collective-permute-done((bf16[32,16,768]{2,1,0:T(8,128)(2,1)S(1)}, bf16[32,16,768]{2,1,0:T(8,128)(2,1)S(1)}, u32[]{:S(2)}, u32[]{:S(2)}) %collective-permute-start.37) | collective-permute-done | bytes 786464 | tf_op jit(solution)/shard_map/ppermute | solution.py:400
  233.0 2.2 collective-permute-done.36
  235.7 6.2 %update.1 = (bf16[1024,768]{1,0:T(8,128)(2,1)}, f32[1024,6]{1,0:T(8,128)S(1)}, f32[1024,768]{1,0:T(8,128)}, f32[1024,768]{1,0:T(8,128)}, f32[1024,768]{1,0:T(8,128)}) custom-call(bf16[1024,768]{1,0:T(8,128)(2,1)S(1)} %bitcast.51, bf16[1024,768]{1,0:T(8,128)(2,1)S(1)} %bitcast.47, bf16[1024,768]{1,0:T(8,128)(2,1)S(1)} %bitcast.46, f32[1024,768]{1,0:T(8,128)S(1)} %bitcast.48, ...), custom_call_target="tpu_custom_call" | custom-call | flops 15728640 | bytes 25165824 | tf_op jit(solution)/shard_map/update/pallas_call | solution.py:378
  (130 shorter events, 35.0 us)
Async XLA Ops:
  3.8 7.6 %collective-permute-start.1 = (bf16[144,768]{1,0:T(8,128)(2,1)S(1)}, bf16[144,768]{1,0:T(8,128)(2,1)S(1)}, u32[]{:S(2)}, u32[]{:S(2)}) collective-permute-start(bf16[144,768]{1,0:T(8,128)(2,1)S(1)} %get-tuple-element.93), channel_id=1, source_target_pairs={{0,24},{1,25},{2,26},{3,27},{4,28},{5,29},{6,30},{7,31},{8,0},{9,1... | collective-permute-start | bytes 663560 | tf_op jit(solution)/shard_map/ppermute | solution.py:414
  4.4 7.6 %collective-permute-start.2 = (bf16[144,768]{1,0:T(8,128)(2,1)S(1)}, bf16[144,768]{1,0:T(8,128)(2,1)S(1)}, u32[]{:S(2)}, u32[]{:S(2)}) collective-permute-start(bf16[144,768]{1,0:T(8,128)(2,1)S(1)} %get-tuple-element.93), channel_id=1, source_target_pairs={{0,8},{1,9},{2,10},{3,11},{4,12},{5,13},{6,14},{7,15},{8,16},{9,17... | collective-permute-start | bytes 663560 | tf_op jit(solution)/shard_map/ppermute | solution.py:414
  11.4 11.8 %collective-permute-start.4 = (bf16[72,768]{1,0:T(8,128)(2,1)S(1)}, bf16[72,768]{1,0:T(8,128)(2,1)S(1)}, u32[]{:S(2)}, u32[]{:S(2)}) collective-permute-start(bf16[72,768]{1,0:T(8,128)(2,1)S(1)} %slice.173), channel_id=1, source_target_pairs={{0,24},{1,25},{2,26},{3,27},{4,28},{5,29},{6,30},{7,31},{8,0},{9,1... | collective-permute-start | bytes 331784 | tf_op jit(solution)/shard_map/ppermute | solution.py:414
  12.0 11.2 %collective-permute-start.3 = (bf16[72,768]{1,0:T(8,128)(2,1)S(1)}, bf16[72,768]{1,0:T(8,128)(2,1)S(1)}, u32[]{:S(2)}, u32[]{:S(2)}) collective-permute-start(bf16[72,768]{1,0:T(8,128)(2,1)S(1)} %slice.172), channel_id=1, source_target_pairs={{0,8},{1,9},{2,10},{3,11},{4,12},{5,13},{6,14},{7,15},{8,16},{9,17... | collective-permute-start | bytes 331784 | tf_op jit(solution)/shard_map/ppermute | solution.py:414
  20.0 36.9 %collective-permute-start.10 = (bf16[64,16,768]{2,1,0:T(8,128)(2,1)}, bf16[64,16,768]{2,1,0:T(8,128)(2,1)}, u32[]{:S(2)}, u32[]{:S(2)}) collective-permute-start(bf16[64,16,768]{2,1,0:T(8,128)(2,1)} %bitcast.55), channel_id=1, source_target_pairs={{0,32},{32,64},{64,96},{96,0},{1,33},{33,65},{65,97},{97,1},{2,34}... | collective-permute-start | bytes 4718600 | tf_op jit(solution)/shard_map/ppermute | solution.py:400
  21.5 36.5 %collective-permute-start.9 = (bf16[64,16,768]{2,1,0:T(8,128)(2,1)}, bf16[64,16,768]{2,1,0:T(8,128)(2,1)}, u32[]{:S(2)}, u32[]{:S(2)}) collective-permute-start(bf16[64,16,768]{2,1,0:T(8,128)(2,1)} %bitcast.56), channel_id=1, source_target_pairs={{0,96},{32,0},{64,32},{96,64},{1,97},{33,1},{65,33},{97,65},{2,98}... | collective-permute-start | bytes 4718600 | tf_op jit(solution)/shard_map/ppermute | solution.py:400
  23.4 22.6 %collective-permute-start.6 = (bf16[4,144,768]{2,1,0:T(8,128)(2,1)S(1)}, bf16[4,144,768]{2,1,0:T(8,128)(2,1)}, u32[]{:S(2)}, u32[]{:S(2)}) collective-permute-start(bf16[4,144,768]{2,1,0:T(8,128)(2,1)S(1)} %pad_maximum_fusion.2.refs_0_), channel_id=1, source_target_pairs={{0,2},{1,3},{2,4},{3,5},{4,6},{5,7},{6,0},{7,1},{8,10},{9,11},{10,... | collective-permute-start | bytes 2654216 | tf_op jit(solution)/shard_map/ppermute | solution.py:414
  25.3 22.4 %collective-permute-start.5 = (bf16[4,144,768]{2,1,0:T(8,128)(2,1)S(1)}, bf16[4,144,768]{2,1,0:T(8,128)(2,1)}, u32[]{:S(2)}, u32[]{:S(2)}) collective-permute-start(bf16[4,144,768]{2,1,0:T(8,128)(2,1)S(1)} %pad_maximum_fusion.2.refs_0_), channel_id=1, source_target_pairs={{0,6},{1,7},{2,0},{3,1},{4,2},{5,3},{6,4},{7,5},{8,14},{9,15},{10,... | collective-permute-start | bytes 2654216 | tf_op jit(solution)/shard_map/ppermute | solution.py:414
  27.6 35.1 %collective-permute-start.13 = (bf16[4,144,768]{2,1,0:T(8,128)(2,1)S(1)}, bf16[4,144,768]{2,1,0:T(8,128)(2,1)}, u32[]{:S(2)}, u32[]{:S(2)}) collective-permute-start(bf16[4,144,768]{2,1,0:T(8,128)(2,1)S(1)} %pad_maximum_fusion.2.refs_0_), channel_id=1, source_target_pairs={{0,1},{1,0},{2,3},{3,2},{4,5},{5,4},{6,7},{7,6},{8,9},{9,8},{10,11... | collective-permute-start | bytes 2654216 | tf_op jit(solution)/shard_map/ppermute | solution.py:414
  47.7 12.1 %collective-permute-start.7 = (bf16[2,144,768]{2,1,0:T(8,128)(2,1)}, bf16[2,144,768]{2,1,0:T(8,128)(2,1)}, u32[]{:S(2)}, u32[]{:S(2)}) collective-permute-start(bf16[2,144,768]{2,1,0:T(8,128)(2,1)} %slice.177), channel_id=1, source_target_pairs={{0,2},{1,3},{2,4},{3,5},{4,6},{5,7},{6,0},{7,1},{8,10},{9,11},{10,... | collective-permute-start | bytes 1327112 | tf_op jit(solution)/shard_map/ppermute | solution.py:414
  48.8 12.2 %collective-permute-start.8 = (bf16[2,144,768]{2,1,0:T(8,128)(2,1)S(1)}, bf16[2,144,768]{2,1,0:T(8,128)(2,1)}, u32[]{:S(2)}, u32[]{:S(2)}) collective-permute-start(bf16[2,144,768]{2,1,0:T(8,128)(2,1)S(1)} %slice.179), channel_id=1, source_target_pairs={{0,6},{1,7},{2,0},{3,1},{4,2},{5,3},{6,4},{7,5},{8,14},{9,15},{10,... | collective-permute-start | bytes 1327112 | tf_op jit(solution)/shard_map/ppermute | solution.py:414
  56.9 12.2 %collective-permute-start.15 = (bf16[4,144,768]{2,1,0:T(8,128)(2,1)}, bf16[4,144,768]{2,1,0:T(8,128)(2,1)}, u32[]{:S(2)}, u32[]{:S(2)}) collective-permute-start(bf16[4,144,768]{2,1,0:T(8,128)(2,1)} %collective-permute-done.6.refs_2_), channel_id=1, source_target_pairs={{0,1},{1,0},{2,3},{3,2},{4,5},{5,4},{6,7},{7,6},{8,9},{9,8},{10,11... | collective-permute-start | bytes 2654216 | tf_op jit(solution)/shard_map/ppermute | solution.py:414
  58.1 11.0 %collective-permute-start.14 = (bf16[4,144,768]{2,1,0:T(8,128)(2,1)}, bf16[4,144,768]{2,1,0:T(8,128)(2,1)}, u32[]{:S(2)}, u32[]{:S(2)}) collective-permute-start(bf16[4,144,768]{2,1,0:T(8,128)(2,1)} %collective-permute-done.5.refs_1_), channel_id=1, source_target_pairs={{0,1},{1,0},{2,3},{3,2},{4,5},{5,4},{6,7},{7,6},{8,9},{9,8},{10,11... | collective-permute-start | bytes 2654216 | tf_op jit(solution)/shard_map/ppermute | solution.py:414
  59.9 20.8 %collective-permute-start.11 = (bf16[32,16,768]{2,1,0:T(8,128)(2,1)S(1)}, bf16[32,16,768]{2,1,0:T(8,128)(2,1)}, u32[]{:S(2)}, u32[]{:S(2)}) collective-permute-start(bf16[32,16,768]{2,1,0:T(8,128)(2,1)S(1)} %slice.183), channel_id=1, source_target_pairs={{0,32},{32,64},{64,96},{96,0},{1,33},{33,65},{65,97},{97,1},{2,34}... | collective-permute-start | bytes 2359304 | tf_op jit(solution)/shard_map/ppermute | solution.py:400
  62.6 20.4 %collective-permute-start.12 = (bf16[32,16,768]{2,1,0:T(8,128)(2,1)S(1)}, bf16[32,16,768]{2,1,0:T(8,128)(2,1)S(1)}, u32[]{:S(2)}, u32[]{:S(2)}) collective-permute-start(bf16[32,16,768]{2,1,0:T(8,128)(2,1)S(1)} %slice.184), channel_id=1, source_target_pairs={{0,96},{32,0},{64,32},{96,64},{1,97},{33,1},{65,33},{97,65},{2,98}... | collective-permute-start | bytes 2359304 | tf_op jit(solution)/shard_map/ppermute | solution.py:400
  142.7 15.9 %collective-permute-start.20 = (bf16[16,64,768]{2,1,0:T(8,128)(2,1)}, bf16[16,64,768]{2,1,0:T(8,128)(2,1)S(1)}, u32[]{:S(2)}, u32[]{:S(2)}) collective-permute-start(bf16[16,64,768]{2,1,0:T(8,128)(2,1)} %get-tuple-element.27), channel_id=1, source_target_pairs={{0,1},{1,0},{2,3},{3,2},{4,5},{5,4},{6,7},{7,6},{8,9},{9,8},{10,11... | collective-permute-start | bytes 4718600 | tf_op jit(solution)/shard_map/ppermute | solution.py:414
  154.8 11.9 %collective-permute-start.25 = (bf16[16,64,768]{2,1,0:T(8,128)(2,1)}, bf16[16,64,768]{2,1,0:T(8,128)(2,1)S(1)}, u32[]{:S(2)}, u32[]{:S(2)}) collective-permute-start(bf16[16,64,768]{2,1,0:T(8,128)(2,1)} %get-tuple-element.29), channel_id=1, source_target_pairs={{0,1},{1,0},{2,3},{3,2},{4,5},{5,4},{6,7},{7,6},{8,9},{9,8},{10,11... | collective-permute-start | bytes 4718600 | tf_op jit(solution)/shard_map/ppermute | solution.py:414
  154.9 43.5 %collective-permute-start.18 = (bf16[64,16,768]{2,1,0:T(8,128)(2,1)}, bf16[64,16,768]{2,1,0:T(8,128)(2,1)S(1)}, u32[]{:S(2)}, u32[]{:S(2)}) collective-permute-start(bf16[64,16,768]{2,1,0:T(8,128)(2,1)} %get-tuple-element.24), channel_id=1, source_target_pairs={{0,32},{32,64},{64,96},{96,0},{1,33},{33,65},{65,97},{97,1},{2,34}... | collective-permute-start | bytes 4718600 | tf_op jit(solution)/shard_map/ppermute | solution.py:400
  156.8 54.0 %collective-permute-start.19 = (bf16[64,16,768]{2,1,0:T(8,128)(2,1)}, bf16[64,16,768]{2,1,0:T(8,128)(2,1)S(1)}, u32[]{:S(2)}, u32[]{:S(2)}) collective-permute-start(bf16[64,16,768]{2,1,0:T(8,128)(2,1)} %get-tuple-element.25), channel_id=1, source_target_pairs={{0,96},{32,0},{64,32},{96,64},{1,97},{33,1},{65,33},{97,65},{2,98}... | collective-permute-start | bytes 4718600 | tf_op jit(solution)/shard_map/ppermute | solution.py:400
  160.6 14.8 %collective-permute-start.23 = (bf16[4,64,768]{2,1,0:T(8,128)(2,1)S(1)}, bf16[4,64,768]{2,1,0:T(8,128)(2,1)S(1)}, u32[]{:S(2)}, u32[]{:S(2)}) collective-permute-start(bf16[4,64,768]{2,1,0:T(8,128)(2,1)S(1)} %get-tuple-element.84), channel_id=1, source_target_pairs={{0,24},{1,25},{2,26},{3,27},{4,28},{5,29},{6,30},{7,31},{8,0},{9,1... | collective-permute-start | bytes 1179656 | tf_op jit(solution)/shard_map/ppermute | solution.py:414
  166.7 13.7 %collective-permute-start.21 = (bf16[4,64,768]{2,1,0:T(8,128)(2,1)S(1)}, bf16[4,64,768]{2,1,0:T(8,128)(2,1)S(1)}, u32[]{:S(2)}, u32[]{:S(2)}) collective-permute-start(bf16[4,64,768]{2,1,0:T(8,128)(2,1)S(1)} %get-tuple-element.85), channel_id=1, source_target_pairs={{0,8},{1,9},{2,10},{3,11},{4,12},{5,13},{6,14},{7,15},{8,16},{9,17... | collective-permute-start | bytes 1179656 | tf_op jit(solution)/shard_map/ppermute | solution.py:414
  167.2 13.6 %collective-permute-start.28 = (bf16[4,64,768]{2,1,0:T(8,128)(2,1)S(1)}, bf16[4,64,768]{2,1,0:T(8,128)(2,1)S(1)}, u32[]{:S(2)}, u32[]{:S(2)}) collective-permute-start(bf16[4,64,768]{2,1,0:T(8,128)(2,1)S(1)} %get-tuple-element.80), channel_id=1, source_target_pairs={{0,6},{1,7},{2,0},{3,1},{4,2},{5,3},{6,4},{7,5},{8,14},{9,15},{10,... | collective-permute-start | bytes 1179656 | tf_op jit(solution)/shard_map/ppermute | solution.py:414
  175.3 12.5 %collective-permute-start.26 = (bf16[4,64,768]{2,1,0:T(8,128)(2,1)S(1)}, bf16[4,64,768]{2,1,0:T(8,128)(2,1)S(1)}, u32[]{:S(2)}, u32[]{:S(2)}) collective-permute-start(bf16[4,64,768]{2,1,0:T(8,128)(2,1)S(1)} %get-tuple-element.81), channel_id=1, source_target_pairs={{0,2},{1,3},{2,4},{3,5},{4,6},{5,7},{6,0},{7,1},{8,10},{9,11},{10,... | collective-permute-start | bytes 1179656 | tf_op jit(solution)/shard_map/ppermute | solution.py:414
  180.5 10.8 %collective-permute-start.24 = (bf16[2,64,768]{2,1,0:T(8,128)(2,1)S(1)}, bf16[2,64,768]{2,1,0:T(8,128)(2,1)S(1)}, u32[]{:S(2)}, u32[]{:S(2)}) collective-permute-start(bf16[2,64,768]{2,1,0:T(8,128)(2,1)S(1)} %get-tuple-element.82), channel_id=1, source_target_pairs={{0,24},{1,25},{2,26},{3,27},{4,28},{5,29},{6,30},{7,31},{8,0},{9,1... | collective-permute-start | bytes 589832 | tf_op jit(solution)/shard_map/ppermute | solution.py:414
  180.8 10.6 %collective-permute-start.22 = (bf16[2,64,768]{2,1,0:T(8,128)(2,1)S(1)}, bf16[2,64,768]{2,1,0:T(8,128)(2,1)S(1)}, u32[]{:S(2)}, u32[]{:S(2)}) collective-permute-start(bf16[2,64,768]{2,1,0:T(8,128)(2,1)S(1)} %get-tuple-element.83), channel_id=1, source_target_pairs={{0,8},{1,9},{2,10},{3,11},{4,12},{5,13},{6,14},{7,15},{8,16},{9,17... | collective-permute-start | bytes 589832 | tf_op jit(solution)/shard_map/ppermute | solution.py:414
  188.0 6.4 %collective-permute-start.29 = (bf16[2,64,768]{2,1,0:T(8,128)(2,1)S(1)}, bf16[2,64,768]{2,1,0:T(8,128)(2,1)S(1)}, u32[]{:S(2)}, u32[]{:S(2)}) collective-permute-start(bf16[2,64,768]{2,1,0:T(8,128)(2,1)S(1)} %get-tuple-element.78), channel_id=1, source_target_pairs={{0,6},{1,7},{2,0},{3,1},{4,2},{5,3},{6,4},{7,5},{8,14},{9,15},{10,... | collective-permute-start | bytes 589832 | tf_op jit(solution)/shard_map/ppermute | solution.py:414
  191.3 7.0 %collective-permute-start.27 = (bf16[2,64,768]{2,1,0:T(8,128)(2,1)S(1)}, bf16[2,64,768]{2,1,0:T(8,128)(2,1)S(1)}, u32[]{:S(2)}, u32[]{:S(2)}) collective-permute-start(bf16[2,64,768]{2,1,0:T(8,128)(2,1)S(1)} %get-tuple-element.79), channel_id=1, source_target_pairs={{0,2},{1,3},{2,4},{3,5},{4,6},{5,7},{6,0},{7,1},{8,10},{9,11},{10,... | collective-permute-start | bytes 589832 | tf_op jit(solution)/shard_map/ppermute | solution.py:414
  210.9 6.9 %collective-permute-start.32 = (bf16[1,64,768]{2,1,0:T(8,128)(2,1)S(1)}, bf16[1,64,768]{2,1,0:T(8,128)(2,1)S(1)}, u32[]{:S(2)}, u32[]{:S(2)}) collective-permute-start(bf16[1,64,768]{2,1,0:T(8,128)(2,1)S(1)} %get-tuple-element.87), channel_id=1, source_target_pairs={{0,6},{1,7},{2,0},{3,1},{4,2},{5,3},{6,4},{7,5},{8,14},{9,15},{10,... | collective-permute-start | bytes 294920 | tf_op jit(solution)/shard_map/ppermute | solution.py:414
  214.1 6.1 %collective-permute-start.31 = (bf16[1,64,768]{2,1,0:T(8,128)(2,1)S(1)}, bf16[1,64,768]{2,1,0:T(8,128)(2,1)S(1)}, u32[]{:S(2)}, u32[]{:S(2)}) collective-permute-start(bf16[1,64,768]{2,1,0:T(8,128)(2,1)S(1)} %get-tuple-element.88), channel_id=1, source_target_pairs={{0,4},{1,5},{2,6},{3,7},{4,0},{5,1},{6,2},{7,3},{8,12},{9,13},{10,... | collective-permute-start | bytes 294920 | tf_op jit(solution)/shard_map/ppermute | solution.py:414
  214.3 18.5 %collective-permute-start.37 = (bf16[32,16,768]{2,1,0:T(8,128)(2,1)S(1)}, bf16[32,16,768]{2,1,0:T(8,128)(2,1)S(1)}, u32[]{:S(2)}, u32[]{:S(2)}) collective-permute-start(bf16[32,16,768]{2,1,0:T(8,128)(2,1)S(1)} %add_convert_fusion.2), channel_id=1, source_target_pairs={{0,96},{32,0},{64,32},{96,64},{1,97},{33,1},{65,33},{97,65},{2,98}... | collective-permute-start | bytes 2359304 | tf_op jit(solution)/shard_map/ppermute | solution.py:400
  215.5 19.7 %collective-permute-start.36 = (bf16[32,16,768]{2,1,0:T(8,128)(2,1)S(1)}, bf16[32,16,768]{2,1,0:T(8,128)(2,1)S(1)}, u32[]{:S(2)}, u32[]{:S(2)}) collective-permute-start(bf16[32,16,768]{2,1,0:T(8,128)(2,1)S(1)} %add_convert_fusion.3), channel_id=1, source_target_pairs={{0,32},{32,64},{64,96},{96,0},{1,33},{33,65},{65,97},{97,1},{2,34}... | collective-permute-start | bytes 2359304 | tf_op jit(solution)/shard_map/ppermute | solution.py:400
  220.2 6.1 %collective-permute-start.34 = (bf16[1,64,768]{2,1,0:T(8,128)(2,1)S(1)}, bf16[1,64,768]{2,1,0:T(8,128)(2,1)S(1)}, u32[]{:S(2)}, u32[]{:S(2)}) collective-permute-start(bf16[1,64,768]{2,1,0:T(8,128)(2,1)S(1)} %get-tuple-element.91), channel_id=1, source_target_pairs={{0,16},{1,17},{2,18},{3,19},{4,20},{5,21},{6,22},{7,23},{8,24},{9,... | collective-permute-start | bytes 294920 | tf_op jit(solution)/shard_map/ppermute | solution.py:414
  (18 other events, 207.4 us)
where the time goes:
time: 243 us
  waiting for transfers between devices  90.1 us (37%)
  Pallas kernels  69.1 us (28%)
  starting transfers between devices  59.5 us (24%)
  local copies, waits for them, and re-layouts  12.5 us (5%)
  other arithmetic  10.6 us (4%)
    pallas_call x1, Pallas kernels, score_and_grads(): pl.pallas_call(score_kernel, out_shape=(share,) * 4 + (label(n_col), labe...  58.7 us
    ppermute x30, waiting for transfers between devices, hop(): return lax.ppermute(value, 'cluster', pairs)  52.8 us
    ppermute x30, starting transfers between devices, hop(): return lax.ppermute(value, 'cluster', pairs)  47.1 us
    ppermute x8, waiting for transfers between devices, shift(): lax.ppermute(value, 'query', [(i, (i + by) % size) for i in range(size)])  37.3 us
    ppermute x8, starting transfers between devices, shift(): lax.ppermute(value, 'query', [(i, (i + by) % size) for i in range(size)])  12.4 us
    pallas_call x1, Pallas kernels, update(): pl.pallas_call(update_kernel, out_shape=(jax.ShapeDtypeStruct((rows, widt...  6.2 us
  transfers between devices with their start and end apart: 38, of which 18 were waited for; matrix products, arithmetic and copies ran while one was open for 8% of the time, Pallas kernels for 2%

commit v1 on v0

--- a/solution.py
+++ b/solution.py
@@ -20,7 +20,6 @@
 
 STEP = 4
 SUB = 512
-ID_ROWS = 16
 SPLIT1, SPLIT2, SPLIT3 = 1,1,1
 
 F32, BF16, I32 = jnp.float32, jnp.bfloat16, jnp.int32
@@ -29,28 +28,24 @@
 
 
 def dequant_kernel(codes_ref, scales_ref, rows_ref):
-    rows, width = codes_ref.shape
-    for blk in range(width // BLK):
-        cols = slice(blk * BLK, (blk + 1) * BLK)
-        scale = jnp.broadcast_to(scales_ref[:, blk : blk + 1], (rows, BLK))
-        rows_ref[:, cols] = (codes_ref[:, cols].astype(F32) * scale).astype(BF16)
+    n_col, quarter, width = codes_ref.shape
+    for col in range(n_col):
+        for blk in range(width // BLK):
+            cols = slice(blk * BLK, (blk + 1) * BLK)
+            scale = jnp.broadcast_to(scales_ref[blk, :, col : col + 1], (quarter, BLK))
+            rows_ref[col, :, cols] = (codes_ref[col, :, cols].astype(F32) * scale).astype(BF16)
 
 
 def dequantize(codes, scales):
-    rows, width = codes.shape
-    tile = min(256, rows)
+    whole = pl.BlockSpec(memory_space=pltpu.VMEM)
     return pl.pallas_call(
         dequant_kernel,
-        out_shape=jax.ShapeDtypeStruct((rows, width), BF16),
-        grid=(rows // tile,),
-        in_specs=[
-            pl.BlockSpec((tile, width), lambda i: (i, 0)),
-            pl.BlockSpec((tile, scales.shape[1]), lambda i: (i, 0)),
-        ],
-        out_specs=pl.BlockSpec((tile, width), lambda i: (i, 0)),
+        out_shape=jax.ShapeDtypeStruct(codes.shape, BF16),
+        in_specs=[whole, whole],
+        out_specs=whole,
         name="dequantize",
         cost_estimate=pl.CostEstimate(
-            flops=rows * width, bytes_accessed=4 * rows * width, transcendentals=0
+            flops=codes.size, bytes_accessed=4 * codes.size, transcendentals=0
         ),
     )(codes, scales)
 
@@ -471,16 +466,10 @@
     my_y = lax.axis_index("query")
     my_col = lax.axis_index("cluster")
 
-    own = dequantize(
-        label_codes.reshape(n_col * quarter, width),
-        label_scales.reshape(n_col * quarter, width // BLK),
-    ).reshape(n_col, quarter, width)
+    own = dequantize(label_codes, label_scales.transpose(2, 1, 0))
     left, right = shift(own, 1), shift(own, -1)
 
-    pair_ids = jnp.concatenate([neg_clusters, hop(neg_clusters, core=1)], axis=1)
-    digits = jnp.concatenate([pair_ids // 64, pair_ids % 64], axis=1).astype(BF16)
-    digits = jnp.pad(digits, ((0, ID_ROWS - 1), (0, width - digits.shape[1])))
-    mine = jnp.concatenate([queries[0], digits])
+    mine = queries[0]
     half_rows = mine.shape[0] // 2
     x_left, x_right = along_x(mine, 1), along_x(mine, -1)
     x_low, x_high = along_x(x_left[:half_rows], 1), along_x(x_right[half_rows:], -1)
@@ -492,8 +481,10 @@
     pieces = pieces + (hop(strip, core=1),)
     pieces = pieces + (hop(z_right, core=1), hop(z_left, core=1))
     pieces = pieces + (hop(z_low, core=1), hop(z_high, core=1))
-    digits = jnp.concatenate([piece[:, -ID_ROWS, :128] for piece in pieces[:5]]).astype(I32)
-    group_ids = (digits[:, :64] * 64 + digits[:, 64:]).reshape(-1)
+    ids = jnp.concatenate([neg_clusters, hop(neg_clusters, core=1)], axis=1)
+    ids = jnp.concatenate([ids] + [along_x(ids, by) for by in (1, -1, 2)])
+    ids = jnp.concatenate([ids] + [along_z(ids, by) for by in (1, -1, 2)])
+    group_ids = ids.reshape(-1)
 
     places = my_col * n_col + jnp.arange(n_col, dtype=I32)
     all_ids = jnp.arange(owner_map.shape[0], dtype=I32)

time: 243 us -> 241 us (level)
  the two profiles are of different devices: /device:TPU:4 before, /device:TPU:0 now
where the time goes in v1:
time: 241 us; the launch traced here: 237 us
  Pallas kernels  87.3 us (36%)
  waiting for transfers between devices  82.5 us (34%)
  starting transfers between devices  52.1 us (22%)
  other arithmetic  8.9 us (4%)
  local copies, waits for them, and re-layouts  4.71 us (2%)
    pallas_call x1, Pallas kernels, score_and_grads(): pl.pallas_call(score_kernel, out_shape=(share,) * 4 + (label(n_col), labe...  77.5 us
    ppermute x36, waiting for transfers between devices, hop(): return lax.ppermute(value, 'cluster', pairs)  62.9 us
    ppermute x36, starting transfers between devices, hop(): return lax.ppermute(value, 'cluster', pairs)  40.7 us
    ppermute x8, waiting for transfers between devices, shift(): lax.ppermute(value, 'query', [(i, (i + by) % size) for i in range(size)])  19.6 us
    ppermute x8, starting transfers between devices, shift(): lax.ppermute(value, 'query', [(i, (i + by) % size) for i in range(size)])  11.4 us
    pallas_call x1, Pallas kernels, update(): pl.pallas_call(update_kernel, out_shape=(jax.ShapeDtypeStruct((rows, widt...  6.24 us
  transfers between devices with their start and end apart: 44, of which 21 were waited for; matrix products, arithmetic and copies ran while one was open for 5% of the time, Pallas kernels for 2%

profile of v1, /device:TPU:0, one launch (start us, length us, event | category | flops | bytes accessed | tf_op | source)
XLA Modules:
  0.0 236.7 jit_solution(14105102905382947644)
XLA Ops:
  3.9 4.7 %collective-permute-done.12 = bf16[128,768]{1,0:T(8,128)(2,1)S(1)} collective-permute-done((bf16[128,768]{1,0:T(8,128)(2,1)}, bf16[128,768]{1,0:T(8,128)(2,1)S(1)}, u32[]{:S(2)}, u32[]{:S(2)}) %collective-permute-start.12) | collective-permute-done | bytes 196640 | tf_op jit(solution)/shard_map/ppermute | solution.py:409
  9.2 2.8 %collective-permute-start.14 = (bf16[64,768]{1,0:T(8,128)(2,1)S(1)}, bf16[64,768]{1,0:T(8,128)(2,1)S(1)}, u32[]{:S(2)}, u32[]{:S(2)}) collective-permute-start(bf16[64,768]{1,0:T(8,128)(2,1)S(1)} %slice.147), channel_id=1, source_target_pairs={{0,24},{1,25},{2,26},{3,27},{4,28},{5,29},{6,30},{7,31},{8,0},{9,1... | collective-permute-start | bytes 294920 | tf_op jit(solution)/shard_map/ppermute | solution.py:409
  12.1 3.6 %dequantize.1.own_hbm = bf16[64,16,768]{2,1,0:T(8,128)(2,1)} custom-call(bf16[64,16,768]{2,1,0:T(8,128)(2,1)} %codes_ref.1, f32[6,16,64]{2,1,0:T(8,128)} %bitcast.32), custom_call_target="tpu_custom_call" | custom-call | flops 786432 | bytes 3145728 | tf_op jit(solution)/shard_map/dequantize/pallas_call | solution.py:41
  15.7 1.8 collective-permute-start.8
  19.1 2.2 collective-permute-start.16
  21.2 2.2 collective-permute-start.15
  25.3 4.5 %collective-permute-done.3 = s32[1,64]{1,0:T(1,128)S(1)} collective-permute-done((s32[1,64]{1,0:T(1,128)S(1)}, s32[1,64]{1,0:T(1,128)S(1)}, u32[]{:S(2)}, u32[]{:S(2)}) %collective-permute-start.3) | collective-permute-done | bytes 288 | tf_op jit(solution)/shard_map/ppermute | solution.py:409
  30.1 3.2 %collective-permute-done.2 = s32[1,64]{1,0:T(1,128)S(1)} collective-permute-done((s32[1,64]{1,0:T(1,128)S(1)}, s32[1,64]{1,0:T(1,128)S(1)}, u32[]{:S(2)}, u32[]{:S(2)}) %collective-permute-start.2) | collective-permute-done | bytes 288 | tf_op jit(solution)/shard_map/ppermute | solution.py:409
  33.3 4.8 %collective-permute-done.1 = s32[1,64]{1,0:T(1,128)S(1)} collective-permute-done((s32[1,64]{1,0:T(1,128)S(1)}, s32[1,64]{1,0:T(1,128)S(1)}, u32[]{:S(2)}, u32[]{:S(2)}) %collective-permute-start.1) | collective-permute-done | bytes 288 | tf_op jit(solution)/shard_map/ppermute | solution.py:409
  38.2 1.8 collective-permute-start.6
  40.0 3.3 %collective-permute-done.6 = s32[4,64]{1,0:T(4,128)S(1)} collective-permute-done((s32[4,64]{1,0:T(4,128)S(1)}, s32[4,64]{1,0:T(4,128)S(1)}, u32[]{:S(2)}, u32[]{:S(2)}) %collective-permute-start.6) | collective-permute-done | bytes 1056 | tf_op jit(solution)/shard_map/ppermute | solution.py:409
  43.3 2.0 collective-permute-start.5
  48.7 10.4 %collective-permute-done.4 = s32[4,64]{1,0:T(4,128)S(1)} collective-permute-done((s32[4,64]{1,0:T(4,128)S(1)}, s32[4,64]{1,0:T(4,128)S(1)}, u32[]{:S(2)}, u32[]{:S(2)}) %collective-permute-start.4) | collective-permute-done | bytes 1056 | tf_op jit(solution)/shard_map/ppermute | solution.py:409
  59.1 1.7 collective-permute-start.18
  65.2 4.0 %collective-permute-done.18.refs_4_ = bf16[2,128,768]{2,1,0:T(8,128)(2,1)S(1)} collective-permute-done((bf16[2,128,768]{2,1,0:T(8,128)(2,1)S(1)}, bf16[2,128,768]{2,1,0:T(8,128)(2,1)S(1)}, u32[]{:S(2)}, u32[]{:S(2)}) %collective-permute-start.18) | collective-permute-done | bytes 393248 | tf_op jit(solution)/shard_map/ppermute | solution.py:409
  69.2 1.8 collective-permute-start.10
  74.4 11.9 %collective-permute-done.9.low_hbm = bf16[32,16,768]{2,1,0:T(8,128)(2,1)S(1)} collective-permute-done((bf16[32,16,768]{2,1,0:T(8,128)(2,1)S(1)}, bf16[32,16,768]{2,1,0:T(8,128)(2,1)S(1)}, u32[]{:S(2)}, u32[]{:S(2)}) %collective-permute-start.9) | collective-permute-done | bytes 786464 | tf_op jit(solution)/shard_map/ppermute | solution.py:395
  87.7 77.5 %score.1 = (bf16[16,64,768]{2,1,0:T(8,128)(2,1)}, bf16[16,64,768]{2,1,0:T(8,128)(2,1)}, bf16[16,64,768]{2,1,0:T(8,128)(2,1)}, bf16[16,64,768]{2,1,0:T(8,128)(2,1...) custom-call(s32[64]{0:T(128)} %get-tuple-element.57.order_ref, ...), custom_call_target="tpu_custom_call" | custom-call | flops 38654705664 | bytes 25165824 | tf_op jit(solution)/shard_map/score/pallas_call | solution.py:302
  165.8 3.2 %collective-permute-start.25 = (bf16[64,16,768]{2,1,0:T(8,128)(2,1)}, bf16[64,16,768]{2,1,0:T(8,128)(2,1)S(1)}, u32[]{:S(2)}, u32[]{:S(2)}) collective-permute-start(bf16[64,16,768]{2,1,0:T(8,128)(2,1)} %get-tuple-element.25), channel_id=1, source_target_pairs={{0,96},{32,0},{64,32},{96,64},{1,97},{33,1},{65,33},{97,65},{2,98}... | collective-permute-start | bytes 4718600 | tf_op jit(solution)/shard_map/ppermute | solution.py:395
  169.0 1.9 add_convert_fusion.1
  171.1 2.0 collective-permute-start.27
  173.7 8.3 %collective-permute-done.29 = bf16[4,64,768]{2,1,0:T(8,128)(2,1)S(1)} collective-permute-done((bf16[4,64,768]{2,1,0:T(8,128)(2,1)S(1)}, bf16[4,64,768]{2,1,0:T(8,128)(2,1)S(1)}, u32[]{:S(2)}, u32[]{:S(2)}) %collective-permute-start.29) | collective-permute-done | bytes 393248 | tf_op jit(solution)/shard_map/ppermute | solution.py:409
  185.6 7.9 %collective-permute-done.32 = bf16[4,64,768]{2,1,0:T(8,128)(2,1)S(1)} collective-permute-done((bf16[4,64,768]{2,1,0:T(8,128)(2,1)S(1)}, bf16[4,64,768]{2,1,0:T(8,128)(2,1)S(1)}, u32[]{:S(2)}, u32[]{:S(2)}) %collective-permute-start.32) | collective-permute-done | bytes 393248 | tf_op jit(solution)/shard_map/ppermute | solution.py:409
  193.7 2.1 collective-permute-start.33
  196.0 3.3 %collective-permute-done.35 = bf16[2,64,768]{2,1,0:T(8,128)(2,1)S(1)} collective-permute-done((bf16[2,64,768]{2,1,0:T(8,128)(2,1)S(1)}, bf16[2,64,768]{2,1,0:T(8,128)(2,1)S(1)}, u32[]{:S(2)}, u32[]{:S(2)}) %collective-permute-start.35) | collective-permute-done | bytes 196640 | tf_op jit(solution)/shard_map/ppermute | solution.py:409
  200.9 2.7 %collective-permute-done.24 = bf16[64,16,768]{2,1,0:T(8,128)(2,1)S(1)} collective-permute-done((bf16[64,16,768]{2,1,0:T(8,128)(2,1)}, bf16[64,16,768]{2,1,0:T(8,128)(2,1)S(1)}, u32[]{:S(2)}, u32[]{:S(2)}) %collective-permute-start.24) | collective-permute-done | bytes 1572896 | tf_op jit(solution)/shard_map/ppermute | solution.py:395
  203.7 3.2 %collective-permute-start.38 = (bf16[1,64,768]{2,1,0:T(8,128)(2,1)S(1)}, bf16[1,64,768]{2,1,0:T(8,128)(2,1)S(1)}, u32[]{:S(2)}, u32[]{:S(2)}) collective-permute-start(bf16[1,64,768]{2,1,0:T(8,128)(2,1)S(1)} %get-tuple-element.67), channel_id=1, source_target_pairs={{0,6},{1,7},{2,0},{3,1},{4,2},{5,3},{6,4},{7,5},{8,14},{9,15},{10,... | collective-permute-start | bytes 294920 | tf_op jit(solution)/shard_map/ppermute | solution.py:409
  207.3 3.0 %collective-permute-start.43 = (bf16[32,16,768]{2,1,0:T(8,128)(2,1)S(1)}, bf16[32,16,768]{2,1,0:T(8,128)(2,1)S(1)}, u32[]{:S(2)}, u32[]{:S(2)}) collective-permute-start(bf16[32,16,768]{2,1,0:T(8,128)(2,1)S(1)} %add_convert_fusion.2), channel_id=1, source_target_pairs={{0,96},{32,0},{64,32},{96,64},{1,97},{33,1},{65,33},{97,65},{2,98}... | collective-permute-start | bytes 2359304 | tf_op jit(solution)/shard_map/ppermute | solution.py:395
  214.1 7.2 %collective-permute-start.40 = (bf16[1,64,768]{2,1,0:T(8,128)(2,1)S(1)}, bf16[1,64,768]{2,1,0:T(8,128)(2,1)S(1)}, u32[]{:S(2)}, u32[]{:S(2)}) collective-permute-start(bf16[1,64,768]{2,1,0:T(8,128)(2,1)S(1)} %get-tuple-element.71), channel_id=1, source_target_pairs={{0,16},{1,17},{2,18},{3,19},{4,20},{5,21},{6,22},{7,23},{8,24},{9,... | collective-permute-start | bytes 294920 | tf_op jit(solution)/shard_map/ppermute | solution.py:409
  221.4 2.5 %collective-permute-done.40 = bf16[1,64,768]{2,1,0:T(8,128)(2,1)S(1)} collective-permute-done((bf16[1,64,768]{2,1,0:T(8,128)(2,1)S(1)}, bf16[1,64,768]{2,1,0:T(8,128)(2,1)S(1)}, u32[]{:S(2)}, u32[]{:S(2)}) %collective-permute-start.40) | collective-permute-done | bytes 98336 | tf_op jit(solution)/shard_map/ppermute | solution.py:409
  225.9 3.5 %collective-permute-done.42 = bf16[32,16,768]{2,1,0:T(8,128)(2,1)S(1)} collective-permute-done((bf16[32,16,768]{2,1,0:T(8,128)(2,1)S(1)}, bf16[32,16,768]{2,1,0:T(8,128)(2,1)S(1)}, u32[]{:S(2)}, u32[]{:S(2)}) %collective-permute-start.42) | collective-permute-done | bytes 786464 | tf_op jit(solution)/shard_map/ppermute | solution.py:395
  229.6 6.2 %update.1 = (bf16[1024,768]{1,0:T(8,128)(2,1)}, f32[1024,6]{1,0:T(8,128)S(1)}, f32[1024,768]{1,0:T(8,128)}, f32[1024,768]{1,0:T(8,128)}, f32[1024,768]{1,0:T(8,128)}) custom-call(bf16[1024,768]{1,0:T(8,128)(2,1)S(1)} %bitcast.26, bf16[1024,768]{1,0:T(8,128)(2,1)S(1)} %bitcast.22, bf16[1024,768]{1,0:T(8,128)(2,1)S(1)} %bitcast.21, f32[1024,768]{1,0:T(8,128)S(1)} %bitcast.23, ...), custom_call_target="tpu_custom_call" | custom-call | flops 15728640 | bytes 25165824 | tf_op jit(solution)/shard_map/update/pallas_call | solution.py:373
  (147 shorter events, 34.1 us)
Async XLA Ops:
  0.6 8.1 %collective-permute-start.12 = (bf16[128,768]{1,0:T(8,128)(2,1)}, bf16[128,768]{1,0:T(8,128)(2,1)S(1)}, u32[]{:S(2)}, u32[]{:S(2)}) collective-permute-start(bf16[128,768]{1,0:T(8,128)(2,1)} %bitcast.30), channel_id=1, source_target_pairs={{0,8},{1,9},{2,10},{3,11},{4,12},{5,13},{6,14},{7,15},{8,16},{9,17... | collective-permute-start | bytes 589832 | tf_op jit(solution)/shard_map/ppermute | solution.py:409
  8.7 10.2 %collective-permute-start.13 = (bf16[64,768]{1,0:T(8,128)(2,1)S(1)}, bf16[64,768]{1,0:T(8,128)(2,1)S(1)}, u32[]{:S(2)}, u32[]{:S(2)}) collective-permute-start(bf16[64,768]{1,0:T(8,128)(2,1)S(1)} %slice.146), channel_id=1, source_target_pairs={{0,8},{1,9},{2,10},{3,11},{4,12},{5,13},{6,14},{7,15},{8,16},{9,17... | collective-permute-start | bytes 294920 | tf_op jit(solution)/shard_map/ppermute | solution.py:409
  9.2 9.7 %collective-permute-start.14 = (bf16[64,768]{1,0:T(8,128)(2,1)S(1)}, bf16[64,768]{1,0:T(8,128)(2,1)S(1)}, u32[]{:S(2)}, u32[]{:S(2)}) collective-permute-start(bf16[64,768]{1,0:T(8,128)(2,1)S(1)} %slice.147), channel_id=1, source_target_pairs={{0,24},{1,25},{2,26},{3,27},{4,28},{5,29},{6,30},{7,31},{8,0},{9,1... | collective-permute-start | bytes 294920 | tf_op jit(solution)/shard_map/ppermute | solution.py:409
  15.7 46.4 %collective-permute-start.8 = (bf16[64,16,768]{2,1,0:T(8,128)(2,1)}, bf16[64,16,768]{2,1,0:T(8,128)(2,1)}, u32[]{:S(2)}, u32[]{:S(2)}) collective-permute-start(bf16[64,16,768]{2,1,0:T(8,128)(2,1)} %dequantize.1.own_hbm), channel_id=1, source_target_pairs={{0,32},{32,64},{64,96},{96,0},{1,33},{33,65},{65,97},{97,1},{2,34}... | collective-permute-start | bytes 4718600 | tf_op jit(solution)/shard_map/ppermute | solution.py:395
  17.4 46.3 %collective-permute-start.7 = (bf16[64,16,768]{2,1,0:T(8,128)(2,1)}, bf16[64,16,768]{2,1,0:T(8,128)(2,1)}, u32[]{:S(2)}, u32[]{:S(2)}) collective-permute-start(bf16[64,16,768]{2,1,0:T(8,128)(2,1)} %dequantize.1.own_hbm), channel_id=1, source_target_pairs={{0,96},{32,0},{64,32},{96,64},{1,97},{33,1},{65,33},{97,65},{2,98}... | collective-permute-start | bytes 4718600 | tf_op jit(solution)/shard_map/ppermute | solution.py:395
  19.1 24.2 %collective-permute-start.16 = (bf16[4,128,768]{2,1,0:T(8,128)(2,1)S(1)}, bf16[4,128,768]{2,1,0:T(8,128)(2,1)S(1)}, u32[]{:S(2)}, u32[]{:S(2)}) collective-permute-start(bf16[4,128,768]{2,1,0:T(8,128)(2,1)S(1)} %pad_maximum_fusion.2.refs_0_), channel_id=1, source_target_pairs={{0,2},{1,3},{2,4},{3,5},{4,6},{5,7},{6,0},{7,1},{8,10},{9,11},{10,... | collective-permute-start | bytes 2359304 | tf_op jit(solution)/shard_map/ppermute | solution.py:409
  21.2 25.7 %collective-permute-start.15 = (bf16[4,128,768]{2,1,0:T(8,128)(2,1)S(1)}, bf16[4,128,768]{2,1,0:T(8,128)(2,1)S(1)}, u32[]{:S(2)}, u32[]{:S(2)}) collective-permute-start(bf16[4,128,768]{2,1,0:T(8,128)(2,1)S(1)} %pad_maximum_fusion.2.refs_0_), channel_id=1, source_target_pairs={{0,6},{1,7},{2,0},{3,1},{4,2},{5,3},{6,4},{7,5},{8,14},{9,15},{10,... | collective-permute-start | bytes 2359304 | tf_op jit(solution)/shard_map/ppermute | solution.py:409
  43.3 21.8 %collective-permute-start.19 = (bf16[4,128,768]{2,1,0:T(8,128)(2,1)S(1)}, bf16[4,128,768]{2,1,0:T(8,128)(2,1)}, u32[]{:S(2)}, u32[]{:S(2)}) collective-permute-start(bf16[4,128,768]{2,1,0:T(8,128)(2,1)S(1)} %pad_maximum_fusion.2.refs_0_), channel_id=1, source_target_pairs={{0,1},{1,0},{2,3},{3,2},{4,5},{5,4},{6,7},{7,6},{8,9},{9,8},{10,11... | collective-permute-start | bytes 2359304 | tf_op jit(solution)/shard_map/ppermute | solution.py:409
  47.0 14.3 %collective-permute-start.17 = (bf16[2,128,768]{2,1,0:T(8,128)(2,1)S(1)}, bf16[2,128,768]{2,1,0:T(8,128)(2,1)S(1)}, u32[]{:S(2)}, u32[]{:S(2)}) collective-permute-start(bf16[2,128,768]{2,1,0:T(8,128)(2,1)S(1)} %slice.148), channel_id=1, source_target_pairs={{0,2},{1,3},{2,4},{3,5},{4,6},{5,7},{6,0},{7,1},{8,10},{9,11},{10,... | collective-permute-start | bytes 1179656 | tf_op jit(solution)/shard_map/ppermute | solution.py:409
  47.0 12.2 %collective-permute-start.4 = (s32[4,64]{1,0:T(4,128)S(1)}, s32[4,64]{1,0:T(4,128)S(1)}, u32[]{:S(2)}, u32[]{:S(2)}) collective-permute-start(s32[4,64]{1,0:T(4,128)S(1)} %pad_add_fusion), channel_id=1, source_target_pairs={{0,2},{1,3},{2,4},{3,5},{4,6},{5,7},{6,0},{7,1},{8,10},{9,11},{10,... | collective-permute-start | bytes 3080 | tf_op jit(solution)/shard_map/ppermute | solution.py:409
  59.1 10.0 %collective-permute-start.18 = (bf16[2,128,768]{2,1,0:T(8,128)(2,1)S(1)}, bf16[2,128,768]{2,1,0:T(8,128)(2,1)S(1)}, u32[]{:S(2)}, u32[]{:S(2)}) collective-permute-start(bf16[2,128,768]{2,1,0:T(8,128)(2,1)S(1)} %slice.149), channel_id=1, source_target_pairs={{0,6},{1,7},{2,0},{3,1},{4,2},{5,3},{6,4},{7,5},{8,14},{9,15},{10,... | collective-permute-start | bytes 1179656 | tf_op jit(solution)/shard_map/ppermute | solution.py:409
  61.2 10.5 %collective-permute-start.22 = (bf16[2,128,768]{2,1,0:T(8,128)(2,1)S(1)}, bf16[2,128,768]{2,1,0:T(8,128)(2,1)S(1)}, u32[]{:S(2)}, u32[]{:S(2)}) collective-permute-start(bf16[2,128,768]{2,1,0:T(8,128)(2,1)S(1)} %collective-permute-done.17.refs_3_), channel_id=1, source_target_pairs={{0,1},{1,0},{2,3},{3,2},{4,5},{5,4},{6,7},{7,6},{8,9},{9,8},{10,11... | collective-permute-start | bytes 1179656 | tf_op jit(solution)/shard_map/ppermute | solution.py:409
  62.1 12.3 %collective-permute-start.21 = (bf16[4,128,768]{2,1,0:T(8,128)(2,1)S(1)}, bf16[4,128,768]{2,1,0:T(8,128)(2,1)S(1)}, u32[]{:S(2)}, u32[]{:S(2)}) collective-permute-start(bf16[4,128,768]{2,1,0:T(8,128)(2,1)S(1)} %collective-permute-done.16.refs_2_), channel_id=1, source_target_pairs={{0,1},{1,0},{2,3},{3,2},{4,5},{5,4},{6,7},{7,6},{8,9},{9,8},{10,11... | collective-permute-start | bytes 2359304 | tf_op jit(solution)/shard_map/ppermute | solution.py:409
  63.8 10.6 %collective-permute-start.20 = (bf16[4,128,768]{2,1,0:T(8,128)(2,1)S(1)}, bf16[4,128,768]{2,1,0:T(8,128)(2,1)S(1)}, u32[]{:S(2)}, u32[]{:S(2)}) collective-permute-start(bf16[4,128,768]{2,1,0:T(8,128)(2,1)S(1)} %copy-done.11), channel_id=1, source_target_pairs={{0,1},{1,0},{2,3},{3,2},{4,5},{5,4},{6,7},{7,6},{8,9},{9,8},{10,11... | collective-permute-start | bytes 2359304 | tf_op jit(solution)/shard_map/ppermute | solution.py:409
  65.1 21.2 %collective-permute-start.9 = (bf16[32,16,768]{2,1,0:T(8,128)(2,1)S(1)}, bf16[32,16,768]{2,1,0:T(8,128)(2,1)S(1)}, u32[]{:S(2)}, u32[]{:S(2)}) collective-permute-start(bf16[32,16,768]{2,1,0:T(8,128)(2,1)S(1)} %slice.144), channel_id=1, source_target_pairs={{0,32},{32,64},{64,96},{96,0},{1,33},{33,65},{65,97},{97,1},{2,34}... | collective-permute-start | bytes 2359304 | tf_op jit(solution)/shard_map/ppermute | solution.py:395
  69.2 17.6 %collective-permute-start.10 = (bf16[32,16,768]{2,1,0:T(8,128)(2,1)S(1)}, bf16[32,16,768]{2,1,0:T(8,128)(2,1)S(1)}, u32[]{:S(2)}, u32[]{:S(2)}) collective-permute-start(bf16[32,16,768]{2,1,0:T(8,128)(2,1)S(1)} %slice.145), channel_id=1, source_target_pairs={{0,96},{32,0},{64,32},{96,64},{1,97},{33,1},{65,33},{97,65},{2,98}... | collective-permute-start | bytes 2359304 | tf_op jit(solution)/shard_map/ppermute | solution.py:395
  165.3 7.8 %collective-permute-start.31 = (bf16[16,64,768]{2,1,0:T(8,128)(2,1)}, bf16[16,64,768]{2,1,0:T(8,128)(2,1)S(1)}, u32[]{:S(2)}, u32[]{:S(2)}) collective-permute-start(bf16[16,64,768]{2,1,0:T(8,128)(2,1)} %get-tuple-element.29), channel_id=1, source_target_pairs={{0,1},{1,0},{2,3},{3,2},{4,5},{5,4},{6,7},{7,6},{8,9},{9,8},{10,11... | collective-permute-start | bytes 4718600 | tf_op jit(solution)/shard_map/ppermute | solution.py:409
  165.8 37.8 %collective-permute-start.24 = (bf16[64,16,768]{2,1,0:T(8,128)(2,1)}, bf16[64,16,768]{2,1,0:T(8,128)(2,1)S(1)}, u32[]{:S(2)}, u32[]{:S(2)}) collective-permute-start(bf16[64,16,768]{2,1,0:T(8,128)(2,1)} %get-tuple-element.24), channel_id=1, source_target_pairs={{0,32},{32,64},{64,96},{96,0},{1,33},{33,65},{65,97},{97,1},{2,34}... | collective-permute-start | bytes 4718600 | tf_op jit(solution)/shard_map/ppermute | solution.py:395
  165.8 37.8 %collective-permute-start.25 = (bf16[64,16,768]{2,1,0:T(8,128)(2,1)}, bf16[64,16,768]{2,1,0:T(8,128)(2,1)S(1)}, u32[]{:S(2)}, u32[]{:S(2)}) collective-permute-start(bf16[64,16,768]{2,1,0:T(8,128)(2,1)} %get-tuple-element.25), channel_id=1, source_target_pairs={{0,96},{32,0},{64,32},{96,64},{1,97},{33,1},{65,33},{97,65},{2,98}... | collective-permute-start | bytes 4718600 | tf_op jit(solution)/shard_map/ppermute | solution.py:395
  171.0 11.1 %collective-permute-start.29 = (bf16[4,64,768]{2,1,0:T(8,128)(2,1)S(1)}, bf16[4,64,768]{2,1,0:T(8,128)(2,1)S(1)}, u32[]{:S(2)}, u32[]{:S(2)}) collective-permute-start(bf16[4,64,768]{2,1,0:T(8,128)(2,1)S(1)} %get-tuple-element.64), channel_id=1, source_target_pairs={{0,24},{1,25},{2,26},{3,27},{4,28},{5,29},{6,30},{7,31},{8,0},{9,1... | collective-permute-start | bytes 1179656 | tf_op jit(solution)/shard_map/ppermute | solution.py:409
  171.1 12.3 %collective-permute-start.27 = (bf16[4,64,768]{2,1,0:T(8,128)(2,1)S(1)}, bf16[4,64,768]{2,1,0:T(8,128)(2,1)S(1)}, u32[]{:S(2)}, u32[]{:S(2)}) collective-permute-start(bf16[4,64,768]{2,1,0:T(8,128)(2,1)S(1)} %get-tuple-element.65), channel_id=1, source_target_pairs={{0,8},{1,9},{2,10},{3,11},{4,12},{5,13},{6,14},{7,15},{8,16},{9,17... | collective-permute-start | bytes 1179656 | tf_op jit(solution)/shard_map/ppermute | solution.py:409
  173.6 10.5 %collective-permute-start.34 = (bf16[4,64,768]{2,1,0:T(8,128)(2,1)S(1)}, bf16[4,64,768]{2,1,0:T(8,128)(2,1)S(1)}, u32[]{:S(2)}, u32[]{:S(2)}) collective-permute-start(bf16[4,64,768]{2,1,0:T(8,128)(2,1)S(1)} %get-tuple-element.60), channel_id=1, source_target_pairs={{0,6},{1,7},{2,0},{3,1},{4,2},{5,3},{6,4},{7,5},{8,14},{9,15},{10,... | collective-permute-start | bytes 1179656 | tf_op jit(solution)/shard_map/ppermute | solution.py:409
  182.1 11.4 %collective-permute-start.32 = (bf16[4,64,768]{2,1,0:T(8,128)(2,1)S(1)}, bf16[4,64,768]{2,1,0:T(8,128)(2,1)S(1)}, u32[]{:S(2)}, u32[]{:S(2)}) collective-permute-start(bf16[4,64,768]{2,1,0:T(8,128)(2,1)S(1)} %get-tuple-element.61), channel_id=1, source_target_pairs={{0,2},{1,3},{2,4},{3,5},{4,6},{5,7},{6,0},{7,1},{8,10},{9,11},{10,... | collective-permute-start | bytes 1179656 | tf_op jit(solution)/shard_map/ppermute | solution.py:409
  183.5 10.3 %collective-permute-start.30 = (bf16[2,64,768]{2,1,0:T(8,128)(2,1)S(1)}, bf16[2,64,768]{2,1,0:T(8,128)(2,1)S(1)}, u32[]{:S(2)}, u32[]{:S(2)}) collective-permute-start(bf16[2,64,768]{2,1,0:T(8,128)(2,1)S(1)} %get-tuple-element.62), channel_id=1, source_target_pairs={{0,24},{1,25},{2,26},{3,27},{4,28},{5,29},{6,30},{7,31},{8,0},{9,1... | collective-permute-start | bytes 589832 | tf_op jit(solution)/shard_map/ppermute | solution.py:409
  184.2 11.6 %collective-permute-start.28 = (bf16[2,64,768]{2,1,0:T(8,128)(2,1)S(1)}, bf16[2,64,768]{2,1,0:T(8,128)(2,1)S(1)}, u32[]{:S(2)}, u32[]{:S(2)}) collective-permute-start(bf16[2,64,768]{2,1,0:T(8,128)(2,1)S(1)} %get-tuple-element.63), channel_id=1, source_target_pairs={{0,8},{1,9},{2,10},{3,11},{4,12},{5,13},{6,14},{7,15},{8,16},{9,17... | collective-permute-start | bytes 589832 | tf_op jit(solution)/shard_map/ppermute | solution.py:409
  203.7 8.7 %collective-permute-start.38 = (bf16[1,64,768]{2,1,0:T(8,128)(2,1)S(1)}, bf16[1,64,768]{2,1,0:T(8,128)(2,1)S(1)}, u32[]{:S(2)}, u32[]{:S(2)}) collective-permute-start(bf16[1,64,768]{2,1,0:T(8,128)(2,1)S(1)} %get-tuple-element.67), channel_id=1, source_target_pairs={{0,6},{1,7},{2,0},{3,1},{4,2},{5,3},{6,4},{7,5},{8,14},{9,15},{10,... | collective-permute-start | bytes 294920 | tf_op jit(solution)/shard_map/ppermute | solution.py:409
  206.9 7.2 %collective-permute-start.37 = (bf16[1,64,768]{2,1,0:T(8,128)(2,1)S(1)}, bf16[1,64,768]{2,1,0:T(8,128)(2,1)S(1)}, u32[]{:S(2)}, u32[]{:S(2)}) collective-permute-start(bf16[1,64,768]{2,1,0:T(8,128)(2,1)S(1)} %get-tuple-element.68), channel_id=1, source_target_pairs={{0,4},{1,5},{2,6},{3,7},{4,0},{5,1},{6,2},{7,3},{8,12},{9,13},{10,... | collective-permute-start | bytes 294920 | tf_op jit(solution)/shard_map/ppermute | solution.py:409
  207.3 18.4 %collective-permute-start.43 = (bf16[32,16,768]{2,1,0:T(8,128)(2,1)S(1)}, bf16[32,16,768]{2,1,0:T(8,128)(2,1)S(1)}, u32[]{:S(2)}, u32[]{:S(2)}) collective-permute-start(bf16[32,16,768]{2,1,0:T(8,128)(2,1)S(1)} %add_convert_fusion.2), channel_id=1, source_target_pairs={{0,96},{32,0},{64,32},{96,64},{1,97},{33,1},{65,33},{97,65},{2,98}... | collective-permute-start | bytes 2359304 | tf_op jit(solution)/shard_map/ppermute | solution.py:395
  210.5 18.8 %collective-permute-start.42 = (bf16[32,16,768]{2,1,0:T(8,128)(2,1)S(1)}, bf16[32,16,768]{2,1,0:T(8,128)(2,1)S(1)}, u32[]{:S(2)}, u32[]{:S(2)}) collective-permute-start(bf16[32,16,768]{2,1,0:T(8,128)(2,1)S(1)} %add_convert_fusion.3), channel_id=1, source_target_pairs={{0,32},{32,64},{64,96},{96,0},{1,33},{33,65},{65,97},{97,1},{2,34}... | collective-permute-start | bytes 2359304 | tf_op jit(solution)/shard_map/ppermute | solution.py:395
  210.8 10.6 %collective-permute-start.39 = (bf16[1,64,768]{2,1,0:T(8,128)(2,1)S(1)}, bf16[1,64,768]{2,1,0:T(8,128)(2,1)S(1)}, u32[]{:S(2)}, u32[]{:S(2)}) collective-permute-start(bf16[1,64,768]{2,1,0:T(8,128)(2,1)S(1)} %get-tuple-element.69), channel_id=1, source_target_pairs={{0,8},{1,9},{2,10},{3,11},{4,12},{5,13},{6,14},{7,15},{8,16},{9,17... | collective-permute-start | bytes 294920 | tf_op jit(solution)/shard_map/ppermute | solution.py:409
  212.4 9.0 %collective-permute-start.41 = (bf16[1,64,768]{2,1,0:T(8,128)(2,1)S(1)}, bf16[1,64,768]{2,1,0:T(8,128)(2,1)S(1)}, u32[]{:S(2)}, u32[]{:S(2)}) collective-permute-start(bf16[1,64,768]{2,1,0:T(8,128)(2,1)S(1)} %get-tuple-element.70), channel_id=1, source_target_pairs={{0,24},{1,25},{2,26},{3,27},{4,28},{5,29},{6,30},{7,31},{8,0},{9,1... | collective-permute-start | bytes 294920 | tf_op jit(solution)/shard_map/ppermute | solution.py:409
  214.1 9.8 %collective-permute-start.40 = (bf16[1,64,768]{2,1,0:T(8,128)(2,1)S(1)}, bf16[1,64,768]{2,1,0:T(8,128)(2,1)S(1)}, u32[]{:S(2)}, u32[]{:S(2)}) collective-permute-start(bf16[1,64,768]{2,1,0:T(8,128)(2,1)S(1)} %get-tuple-element.71), channel_id=1, source_target_pairs={{0,16},{1,17},{2,18},{3,19},{4,20},{5,21},{6,22},{7,23},{8,24},{9,... | collective-permute-start | bytes 294920 | tf_op jit(solution)/shard_map/ppermute | solution.py:409
  (34 other events, 342.1 us)

commit v2 on v1

--- a/solution.py
+++ b/solution.py
@@ -353,11 +353,11 @@
         )
         first = beta_first * first_ref[:, cols] + (1.0 - beta_first) * grad
         second = beta_second * second_ref[:, cols] + (1.0 - beta_second) * grad * grad
-        master = master_ref[:, cols] - learn_rate * (first / fix_first) / (
-            jnp.sqrt(second / fix_second) + adam_eps
+        master = master_ref[:, cols] - first * (learn_rate / fix_first) / (
+            jnp.sqrt(second * (1.0 / fix_second)) + adam_eps
         )
         peak = jnp.max(jnp.abs(master), axis=1, keepdims=True) + scale_eps
-        codes_ref[:, cols] = (master / peak).astype(BF16)
+        codes_ref[:, cols] = (master * (1.0 / peak)).astype(BF16)
         master_out[:, cols] = master
         first_out[:, cols] = first
         second_out[:, cols] = second
@@ -417,16 +417,15 @@
     return send(b, 1), send(c, -1)
 
 
-def ring_close(own, a, d, left, right, send):
+def ring_far(a, d, left, right):
     half = a.shape[0]
-    left_low = send(add(a, left[half:]), 1)
-    right_high = send(add(d, right[:half]), -1)
+    return add(a, left[half:]), add(d, right[:half])
+
+
+def ring_close(own, far, left, right, send):
+    half = far[0].shape[0]
+    left_low, right_high = send(far[0], 1), send(far[1], -1)
     return (own, jnp.concatenate([left_low, left[:half]]), jnp.concatenate([right[half:], right_high]))
-
-
-def ring_sum(value, send):
-    own, a, b, c, d = cut(value)
-    return add(*ring_close(own, a, d, *ring_open(b, c, send), send))
 
 
 def cut(value):
@@ -478,9 +477,6 @@
     far_low, far_high = shift(left[:half], 1), shift(right[half:], -1)
     z_low, z_high = along_z(z_left[:2], 1), along_z(z_right[2:], -1)
     pieces = (strip, z_right, z_left, z_low, z_high)
-    pieces = pieces + (hop(strip, core=1),)
-    pieces = pieces + (hop(z_right, core=1), hop(z_left, core=1))
-    pieces = pieces + (hop(z_low, core=1), hop(z_high, core=1))
     ids = jnp.concatenate([neg_clusters, hop(neg_clusters, core=1)], axis=1)
     ids = jnp.concatenate([ids] + [along_x(ids, by) for by in (1, -1, 2)])
     ids = jnp.concatenate([ids] + [along_z(ids, by) for by in (1, -1, 2)])
@@ -499,6 +495,11 @@
     order = jnp.sum(jnp.where(place, local[None, :], 0), axis=1)
     base = jnp.sum(jnp.where(place, held[None, :], 0), axis=1) * crows
     info = jnp.stack([count, my_y.astype(I32), my_col.astype(I32)])
+    pieces = pieces + (hop(strip, core=1),)
+    pieces = pieces + (hop(z_right, core=1), hop(z_left, core=1))
+    z_low, z_high, order, base, info = lax.optimization_barrier((z_low, z_high, order, base, info))
+    pieces = pieces + (hop(z_low, core=1), hop(z_high, core=1))
+
     *query_parts, label_own, label_a, label_b, label_c, label_d = score_and_grads(
         order,
         base,
@@ -511,10 +512,15 @@
     mine_u, mine_v, part_u, part_v = query_parts
     u = add(mine_u, hop(part_u, core=1))
     v = add(mine_v, hop(part_v, core=1))
-    u = ring_sum(u, along_x)
-    v = ring_sum(v, along_z)
-    label_left, label_right, u, v = lax.optimization_barrier((*label_hops, u, v))
-    label_parts = ring_close(label_own, label_a, label_d, label_left, label_right, shift)
+    u_own, u_a, u_b, u_c, u_d = cut(u)
+    v_own, v_a, v_b, v_c, v_d = cut(v)
+    u_hops, v_hops = ring_open(u_b, u_c, along_x), ring_open(v_b, v_c, along_z)
+    u_far, v_far = ring_far(u_a, u_d, *u_hops), ring_far(v_a, v_d, *v_hops)
+    label_left, label_right, *_ = lax.optimization_barrier((*label_hops, *u_far, *v_far))
+    u = add(*ring_close(u_own, u_far, *u_hops, along_x))
+    v = add(*ring_close(v_own, v_far, *v_hops, along_z))
+    label_sums = ring_far(label_a, label_d, label_left, label_right)
+    label_parts = ring_close(label_own, label_sums, label_left, label_right, shift)
     u = ring_sum_small(u, along_z)
     v = ring_sum_small(v, along_x)
     query_grad = jnp.concatenate([u[0], v[0]]).astype(F32)

time: 241 us -> 239 us (level); the launches traced: 237 us -> 238 us
  waiting for transfers between devices: 82.5 us -> 73.6 us
  local copies, waits for them, and re-layouts: 4.71 us -> 10.3 us
  starting transfers between devices: 52.1 us -> 57.2 us
    ppermute x36, waiting for transfers between devices: 62.9 us -> 53.2 us  [hop(): return lax.ppermute(value, 'cluster', pairs)]
    unnamed x45 -> x57, local copies, waits for them, and re-layouts: 1.85 us -> 6.92 us
    ppermute x36, starting transfers between devices: 40.7 us -> 44.6 us  [hop(): return lax.ppermute(value, 'cluster', pairs)]
  transfers between devices with their start and end apart: 44 -> 44, of which waited for: 21 -> 23; matrix products, arithmetic and copies ran while one was open for 5% -> 5% of each run, Pallas kernels for 2% -> 0%
where the time goes in v2:
time: 239 us; the launch traced here: 238 us
  Pallas kernels  87.2 us (36%)
  waiting for transfers between devices  73.6 us (31%)
  starting transfers between devices  57.2 us (24%)
  local copies, waits for them, and re-layouts  10.3 us (4%)
  other arithmetic  8.76 us (4%)
    pallas_call x1, Pallas kernels, score_and_grads(): pl.pallas_call(score_kernel, out_shape=(share,) * 4 + (label(n_col), labe...  77.5 us
    ppermute x36, waiting for transfers between devices, hop(): return lax.ppermute(value, 'cluster', pairs)  53.2 us
    ppermute x36, starting transfers between devices, hop(): return lax.ppermute(value, 'cluster', pairs)  44.6 us
    ppermute x8, waiting for transfers between devices, shift(): lax.ppermute(value, 'query', [(i, (i + by) % size) for i in range(size)])  20.4 us
    ppermute x8, starting transfers between devices, shift(): lax.ppermute(value, 'query', [(i, (i + by) % size) for i in range(size)])  12.7 us
    unnamed x57, local copies, waits for them, and re-layouts  6.92 us
    pallas_call x1, Pallas kernels, update(): pl.pallas_call(update_kernel, out_shape=(jax.ShapeDtypeStruct((rows, widt...  6.16 us
  transfers between devices with their start and end apart: 44, of which 23 were waited for; matrix products, arithmetic and copies ran while one was open for 5% of the time, Pallas kernels for 0%

profile of v2, /device:TPU:0, one launch (start us, length us, event | category | flops | bytes accessed | tf_op | source)
XLA Modules:
  0.0 238.3 jit_solution(9110671884954446258)
XLA Ops:
  0.6 3.6 %dequantize.1.own_hbm = bf16[64,16,768]{2,1,0:T(8,128)(2,1)} custom-call(bf16[64,16,768]{2,1,0:T(8,128)(2,1)} %codes_ref.1, f32[6,16,64]{2,1,0:T(8,128)} %bitcast.32), custom_call_target="tpu_custom_call" | custom-call | flops 786432 | bytes 3145728 | tf_op jit(solution)/shard_map/dequantize/pallas_call | solution.py:41
  7.4 1.7 collective-permute-start
  9.1 4.3 %collective-permute-done.1 = bf16[128,768]{1,0:T(8,128)(2,1)S(1)} collective-permute-done((bf16[128,768]{1,0:T(8,128)(2,1)S(1)}, bf16[128,768]{1,0:T(8,128)(2,1)S(1)}, u32[]{:S(2)}, u32[]{:S(2)}) %collective-permute-start.1) | collective-permute-done | bytes 196640 | tf_op jit(solution)/shard_map/ppermute | solution.py:409
  13.9 3.0 %collective-permute-start.3 = (bf16[64,768]{1,0:T(8,128)(2,1)S(1)}, bf16[64,768]{1,0:T(8,128)(2,1)S(1)}, u32[]{:S(2)}, u32[]{:S(2)}) collective-permute-start(bf16[64,768]{1,0:T(8,128)(2,1)S(1)} %slice.145), channel_id=1, source_target_pairs={{0,24},{1,25},{2,26},{3,27},{4,28},{5,29},{6,30},{7,31},{8,0},{9,1... | collective-permute-start | bytes 294920 | tf_op jit(solution)/shard_map/ppermute | solution.py:409
  16.9 1.8 collective-permute-start.15
  19.5 4.1 %collective-permute-start.6 = (bf16[4,128,768]{2,1,0:T(8,128)(2,1)S(1)}, bf16[4,128,768]{2,1,0:T(8,128)(2,1)S(1)}, u32[]{:S(2)}, u32[]{:S(2)}) collective-permute-start(bf16[4,128,768]{2,1,0:T(8,128)(2,1)S(1)} %pad_maximum_fusion.2.refs_0_), channel_id=1, source_target_pairs={{0,6},{1,7},{2,0},{3,1},{4,2},{5,3},{6,4},{7,5},{8,14},{9,15},{10,... | collective-permute-start | bytes 2359304 | tf_op jit(solution)/shard_map/ppermute | solution.py:409
  24.9 1.9 collective-permute-start.11
  26.8 3.2 %collective-permute-done.11 = s32[1,64]{1,0:T(1,128)S(1)} collective-permute-done((s32[1,64]{1,0:T(1,128)S(1)}, s32[1,64]{1,0:T(1,128)S(1)}, u32[]{:S(2)}, u32[]{:S(2)}) %collective-permute-start.11) | collective-permute-done | bytes 288 | tf_op jit(solution)/shard_map/ppermute | solution.py:409
  30.0 3.3 %collective-permute-start.10 = (s32[1,64]{1,0:T(1,128)S(1)}, s32[1,64]{1,0:T(1,128)S(1)}, u32[]{:S(2)}, u32[]{:S(2)}) collective-permute-start(s32[1,64]{1,0:T(1,128)S(1)} %pad_add_fusion.1), channel_id=1, source_target_pairs={{0,24},{1,25},{2,26},{3,27},{4,28},{5,29},{6,30},{7,31},{8,0},{9,1... | collective-permute-start | bytes 776 | tf_op jit(solution)/shard_map/ppermute | solution.py:409
  34.6 5.0 %collective-permute-done.9 = s32[1,64]{1,0:T(1,128)S(1)} collective-permute-done((s32[1,64]{1,0:T(1,128)S(1)}, s32[1,64]{1,0:T(1,128)S(1)}, u32[]{:S(2)}, u32[]{:S(2)}) %collective-permute-start.9) | collective-permute-done | bytes 288 | tf_op jit(solution)/shard_map/ppermute | solution.py:409
  39.7 1.9 collective-permute-start.14
  41.6 3.2 %collective-permute-done.14 = s32[4,64]{1,0:T(4,128)S(1)} collective-permute-done((s32[4,64]{1,0:T(4,128)S(1)}, s32[4,64]{1,0:T(4,128)S(1)}, u32[]{:S(2)}, u32[]{:S(2)}) %collective-permute-start.14) | collective-permute-done | bytes 1056 | tf_op jit(solution)/shard_map/ppermute | solution.py:409
  44.8 3.2 %collective-permute-start.13 = (s32[4,64]{1,0:T(4,128)S(1)}, s32[4,64]{1,0:T(4,128)S(1)}, u32[]{:S(2)}, u32[]{:S(2)}) collective-permute-start(s32[4,64]{1,0:T(4,128)S(1)} %pad_add_fusion), channel_id=1, source_target_pairs={{0,6},{1,7},{2,0},{3,1},{4,2},{5,3},{6,4},{7,5},{8,14},{9,15},{10,... | collective-permute-start | bytes 3080 | tf_op jit(solution)/shard_map/ppermute | solution.py:409
  49.5 4.8 %collective-permute-done.12 = s32[4,64]{1,0:T(4,128)S(1)} collective-permute-done((s32[4,64]{1,0:T(4,128)S(1)}, s32[4,64]{1,0:T(4,128)S(1)}, u32[]{:S(2)}, u32[]{:S(2)}) %collective-permute-start.12) | collective-permute-done | bytes 1056 | tf_op jit(solution)/shard_map/ppermute | solution.py:409
  54.5 2.1 collective-permute-start.7
  64.0 1.8 collective-permute-done.5.refs_3_
  65.7 1.8 collective-permute-start.18
  72.2 10.4 %collective-permute-done.17.low_hbm = bf16[32,16,768]{2,1,0:T(8,128)(2,1)S(1)} collective-permute-done((bf16[32,16,768]{2,1,0:T(8,128)(2,1)S(1)}, bf16[32,16,768]{2,1,0:T(8,128)(2,1)S(1)}, u32[]{:S(2)}, u32[]{:S(2)}) %collective-permute-start.17) | collective-permute-done | bytes 786464 | tf_op jit(solution)/shard_map/ppermute | solution.py:395
  84.4 77.5 %score.1 = (bf16[16,64,768]{2,1,0:T(8,128)(2,1)}, bf16[16,64,768]{2,1,0:T(8,128)(2,1)}, bf16[16,64,768]{2,1,0:T(8,128)(2,1)}, bf16[16,64,768]{2,1,0:T(8,128)(2,1...) custom-call(s32[64]{0:T(128)} %get-tuple-element.27.order_ref, ...), custom_call_target="tpu_custom_call" | custom-call | flops 38654705664 | bytes 25165824 | tf_op jit(solution)/shard_map/score/pallas_call | solution.py:302
  162.5 3.2 %collective-permute-start.41 = (bf16[64,16,768]{2,1,0:T(8,128)(2,1)}, bf16[64,16,768]{2,1,0:T(8,128)(2,1)S(1)}, u32[]{:S(2)}, u32[]{:S(2)}) collective-permute-start(bf16[64,16,768]{2,1,0:T(8,128)(2,1)} %get-tuple-element.39), channel_id=1, source_target_pairs={{0,96},{32,0},{64,32},{96,64},{1,97},{33,1},{65,33},{97,65},{2,98}... | collective-permute-start | bytes 4718600 | tf_op jit(solution)/shard_map/ppermute | solution.py:395
  165.8 1.9 add_convert_fusion.1
  167.8 2.0 collective-permute-start.25
  170.5 8.4 %collective-permute-done.27 = bf16[4,64,768]{2,1,0:T(8,128)(2,1)S(1)} collective-permute-done((bf16[4,64,768]{2,1,0:T(8,128)(2,1)S(1)}, bf16[4,64,768]{2,1,0:T(8,128)(2,1)S(1)}, u32[]{:S(2)}, u32[]{:S(2)}) %collective-permute-start.27) | collective-permute-done | bytes 393248 | tf_op jit(solution)/shard_map/ppermute | solution.py:409
  182.3 7.9 %collective-permute-done.33 = bf16[4,64,768]{2,1,0:T(8,128)(2,1)S(1)} collective-permute-done((bf16[4,64,768]{2,1,0:T(8,128)(2,1)S(1)}, bf16[4,64,768]{2,1,0:T(8,128)(2,1)S(1)}, u32[]{:S(2)}, u32[]{:S(2)}) %collective-permute-start.33) | collective-permute-done | bytes 393248 | tf_op jit(solution)/shard_map/ppermute | solution.py:409
  190.4 9.9 %collective-permute-done.40 = bf16[64,16,768]{2,1,0:T(8,128)(2,1)S(1)} collective-permute-done((bf16[64,16,768]{2,1,0:T(8,128)(2,1)}, bf16[64,16,768]{2,1,0:T(8,128)(2,1)S(1)}, u32[]{:S(2)}, u32[]{:S(2)}) %collective-permute-start.40) | collective-permute-done | bytes 1572896 | tf_op jit(solution)/shard_map/ppermute | solution.py:395
  202.2 2.5 %collective-permute-start.43 = (bf16[32,16,768]{2,1,0:T(8,128)(2,1)S(1)}, bf16[32,16,768]{2,1,0:T(8,128)(2,1)S(1)}, u32[]{:S(2)}, u32[]{:S(2)}) collective-permute-start(bf16[32,16,768]{2,1,0:T(8,128)(2,1)S(1)} %add_convert_fusion.2), channel_id=1, source_target_pairs={{0,96},{32,0},{64,32},{96,64},{1,97},{33,1},{65,33},{97,65},{2,98}... | collective-permute-start | bytes 2359304 | tf_op jit(solution)/shard_map/ppermute | solution.py:395
  206.0 3.2 %collective-permute-start.31 = (bf16[1,64,768]{2,1,0:T(8,128)(2,1)S(1)}, bf16[1,64,768]{2,1,0:T(8,128)(2,1)S(1)}, u32[]{:S(2)}, u32[]{:S(2)}) collective-permute-start(bf16[1,64,768]{2,1,0:T(8,128)(2,1)S(1)} %get-tuple-element.73), channel_id=1, source_target_pairs={{0,6},{1,7},{2,0},{3,1},{4,2},{5,3},{6,4},{7,5},{8,14},{9,15},{10,... | collective-permute-start | bytes 294920 | tf_op jit(solution)/shard_map/ppermute | solution.py:409
  209.4 2.6 %collective-permute-done.29 = bf16[1,64,768]{2,1,0:T(8,128)(2,1)S(1)} collective-permute-done((bf16[1,64,768]{2,1,0:T(8,128)(2,1)S(1)}, bf16[1,64,768]{2,1,0:T(8,128)(2,1)S(1)}, u32[]{:S(2)}, u32[]{:S(2)}) %collective-permute-start.29) | collective-permute-done | bytes 98336 | tf_op jit(solution)/shard_map/ppermute | solution.py:409
  212.4 2.9 %collective-permute-start.39 = (bf16[1,64,768]{2,1,0:T(8,128)(2,1)S(1)}, bf16[1,64,768]{2,1,0:T(8,128)(2,1)S(1)}, u32[]{:S(2)}, u32[]{:S(2)}) collective-permute-start(bf16[1,64,768]{2,1,0:T(8,128)(2,1)S(1)} %get-tuple-element.76), channel_id=1, source_target_pairs={{0,24},{1,25},{2,26},{3,27},{4,28},{5,29},{6,30},{7,31},{8,0},{9,1... | collective-permute-start | bytes 294920 | tf_op jit(solution)/shard_map/ppermute | solution.py:409
  215.3 9.6 %collective-permute-start.38 = (bf16[1,64,768]{2,1,0:T(8,128)(2,1)S(1)}, bf16[1,64,768]{2,1,0:T(8,128)(2,1)S(1)}, u32[]{:S(2)}, u32[]{:S(2)}) collective-permute-start(bf16[1,64,768]{2,1,0:T(8,128)(2,1)S(1)} %get-tuple-element.77), channel_id=1, source_target_pairs={{0,16},{1,17},{2,18},{3,19},{4,20},{5,21},{6,22},{7,23},{8,24},{9,... | collective-permute-start | bytes 294920 | tf_op jit(solution)/shard_map/ppermute | solution.py:409
  225.0 2.5 %collective-permute-done.38 = bf16[1,64,768]{2,1,0:T(8,128)(2,1)S(1)} collective-permute-done((bf16[1,64,768]{2,1,0:T(8,128)(2,1)S(1)}, bf16[1,64,768]{2,1,0:T(8,128)(2,1)S(1)}, u32[]{:S(2)}, u32[]{:S(2)}) %collective-permute-start.38) | collective-permute-done | bytes 98336 | tf_op jit(solution)/shard_map/ppermute | solution.py:409
  231.2 6.2 %update.1 = (bf16[1024,768]{1,0:T(8,128)(2,1)}, f32[1024,6]{1,0:T(8,128)S(1)}, f32[1024,768]{1,0:T(8,128)}, f32[1024,768]{1,0:T(8,128)}, f32[1024,768]{1,0:T(8,128)}) custom-call(bf16[1024,768]{1,0:T(8,128)(2,1)S(1)} %bitcast.26, bf16[1024,768]{1,0:T(8,128)(2,1)S(1)} %bitcast.22, bf16[1024,768]{1,0:T(8,128)(2,1)S(1)} %bitcast.21, f32[1024,768]{1,0:T(8,128)S(1)} %bitcast.23, ...), custom_call_target="tpu_custom_call" | custom-call | flops 15728640 | bytes 25165824 | tf_op jit(solution)/shard_map/update/pallas_call | solution.py:373
  (165 shorter events, 35.6 us)
Async XLA Ops:
  4.2 53.3 %collective-permute-start.16 = (bf16[64,16,768]{2,1,0:T(8,128)(2,1)}, bf16[64,16,768]{2,1,0:T(8,128)(2,1)}, u32[]{:S(2)}, u32[]{:S(2)}) collective-permute-start(bf16[64,16,768]{2,1,0:T(8,128)(2,1)} %dequantize.1.own_hbm), channel_id=1, source_target_pairs={{0,32},{32,64},{64,96},{96,0},{1,33},{33,65},{65,97},{97,1},{2,34}... | collective-permute-start | bytes 4718600 | tf_op jit(solution)/shard_map/ppermute | solution.py:395
  5.9 7.6 %collective-permute-start.1 = (bf16[128,768]{1,0:T(8,128)(2,1)S(1)}, bf16[128,768]{1,0:T(8,128)(2,1)S(1)}, u32[]{:S(2)}, u32[]{:S(2)}) collective-permute-start(bf16[128,768]{1,0:T(8,128)(2,1)S(1)} %bitcast.30), channel_id=1, source_target_pairs={{0,8},{1,9},{2,10},{3,11},{4,12},{5,13},{6,14},{7,15},{8,16},{9,17... | collective-permute-start | bytes 589832 | tf_op jit(solution)/shard_map/ppermute | solution.py:409
  7.4 6.4 %collective-permute-start = (bf16[128,768]{1,0:T(8,128)(2,1)S(1)}, bf16[128,768]{1,0:T(8,128)(2,1)S(1)}, u32[]{:S(2)}, u32[]{:S(2)}) collective-permute-start(bf16[128,768]{1,0:T(8,128)(2,1)S(1)} %bitcast.31), channel_id=1, source_target_pairs={{0,24},{1,25},{2,26},{3,27},{4,28},{5,29},{6,30},{7,31},{8,0},{9,1... | collective-permute-start | bytes 589832 | tf_op jit(solution)/shard_map/ppermute | solution.py:409
  16.9 43.1 %collective-permute-start.15 = (bf16[64,16,768]{2,1,0:T(8,128)(2,1)}, bf16[64,16,768]{2,1,0:T(8,128)(2,1)}, u32[]{:S(2)}, u32[]{:S(2)}) collective-permute-start(bf16[64,16,768]{2,1,0:T(8,128)(2,1)} %dequantize.1.own_hbm), channel_id=1, source_target_pairs={{0,96},{32,0},{64,32},{96,64},{1,97},{33,1},{65,33},{97,65},{2,98}... | collective-permute-start | bytes 4718600 | tf_op jit(solution)/shard_map/ppermute | solution.py:395
  19.5 35.0 %collective-permute-start.6 = (bf16[4,128,768]{2,1,0:T(8,128)(2,1)S(1)}, bf16[4,128,768]{2,1,0:T(8,128)(2,1)S(1)}, u32[]{:S(2)}, u32[]{:S(2)}) collective-permute-start(bf16[4,128,768]{2,1,0:T(8,128)(2,1)S(1)} %pad_maximum_fusion.2.refs_0_), channel_id=1, source_target_pairs={{0,6},{1,7},{2,0},{3,1},{4,2},{5,3},{6,4},{7,5},{8,14},{9,15},{10,... | collective-permute-start | bytes 2359304 | tf_op jit(solution)/shard_map/ppermute | solution.py:409
  23.6 33.0 %collective-permute-start.4 = (bf16[4,128,768]{2,1,0:T(8,128)(2,1)S(1)}, bf16[4,128,768]{2,1,0:T(8,128)(2,1)S(1)}, u32[]{:S(2)}, u32[]{:S(2)}) collective-permute-start(bf16[4,128,768]{2,1,0:T(8,128)(2,1)S(1)} %pad_maximum_fusion.2.refs_0_), channel_id=1, source_target_pairs={{0,2},{1,3},{2,4},{3,5},{4,6},{5,7},{6,0},{7,1},{8,10},{9,11},{10,... | collective-permute-start | bytes 2359304 | tf_op jit(solution)/shard_map/ppermute | solution.py:409
  54.5 7.8 %collective-permute-start.7 = (bf16[2,128,768]{2,1,0:T(8,128)(2,1)S(1)}, bf16[2,128,768]{2,1,0:T(8,128)(2,1)S(1)}, u32[]{:S(2)}, u32[]{:S(2)}) collective-permute-start(bf16[2,128,768]{2,1,0:T(8,128)(2,1)S(1)} %slice.147), channel_id=1, source_target_pairs={{0,6},{1,7},{2,0},{3,1},{4,2},{5,3},{6,4},{7,5},{8,14},{9,15},{10,... | collective-permute-start | bytes 1179656 | tf_op jit(solution)/shard_map/ppermute | solution.py:409
  56.7 9.1 %collective-permute-start.5 = (bf16[2,128,768]{2,1,0:T(8,128)(2,1)S(1)}, bf16[2,128,768]{2,1,0:T(8,128)(2,1)S(1)}, u32[]{:S(2)}, u32[]{:S(2)}) collective-permute-start(bf16[2,128,768]{2,1,0:T(8,128)(2,1)S(1)} %slice.146), channel_id=1, source_target_pairs={{0,2},{1,3},{2,4},{3,5},{4,6},{5,7},{6,0},{7,1},{8,10},{9,11},{10,... | collective-permute-start | bytes 1179656 | tf_op jit(solution)/shard_map/ppermute | solution.py:409
  57.5 12.4 %collective-permute-start.19 = (bf16[4,128,768]{2,1,0:T(8,128)(2,1)S(1)}, bf16[4,128,768]{2,1,0:T(8,128)(2,1)S(1)}, u32[]{:S(2)}, u32[]{:S(2)}) collective-permute-start(bf16[4,128,768]{2,1,0:T(8,128)(2,1)S(1)} %pad_maximum_fusion.2.refs_0_), channel_id=1, source_target_pairs={{0,1},{1,0},{2,3},{3,2},{4,5},{5,4},{6,7},{7,6},{8,9},{9,8},{10,11... | collective-permute-start | bytes 2359304 | tf_op jit(solution)/shard_map/ppermute | solution.py:409
  57.5 12.4 %collective-permute-start.20 = (bf16[4,128,768]{2,1,0:T(8,128)(2,1)S(1)}, bf16[4,128,768]{2,1,0:T(8,128)(2,1)S(1)}, u32[]{:S(2)}, u32[]{:S(2)}) collective-permute-start(bf16[4,128,768]{2,1,0:T(8,128)(2,1)S(1)} %collective-permute-done.6.refs_1_), channel_id=1, source_target_pairs={{0,1},{1,0},{2,3},{3,2},{4,5},{5,4},{6,7},{7,6},{8,9},{9,8},{10,11... | collective-permute-start | bytes 2359304 | tf_op jit(solution)/shard_map/ppermute | solution.py:409
  60.0 12.2 %collective-permute-start.21 = (bf16[4,128,768]{2,1,0:T(8,128)(2,1)S(1)}, bf16[4,128,768]{2,1,0:T(8,128)(2,1)S(1)}, u32[]{:S(2)}, u32[]{:S(2)}) collective-permute-start(bf16[4,128,768]{2,1,0:T(8,128)(2,1)S(1)} %collective-permute-done.4.refs_2_), channel_id=1, source_target_pairs={{0,1},{1,0},{2,3},{3,2},{4,5},{5,4},{6,7},{7,6},{8,9},{9,8},{10,11... | collective-permute-start | bytes 2359304 | tf_op jit(solution)/shard_map/ppermute | solution.py:409
  62.4 20.2 %collective-permute-start.17 = (bf16[32,16,768]{2,1,0:T(8,128)(2,1)S(1)}, bf16[32,16,768]{2,1,0:T(8,128)(2,1)S(1)}, u32[]{:S(2)}, u32[]{:S(2)}) collective-permute-start(bf16[32,16,768]{2,1,0:T(8,128)(2,1)S(1)} %slice.148), channel_id=1, source_target_pairs={{0,32},{32,64},{64,96},{96,0},{1,33},{33,65},{65,97},{97,1},{2,34}... | collective-permute-start | bytes 2359304 | tf_op jit(solution)/shard_map/ppermute | solution.py:395
  65.7 16.9 %collective-permute-start.18 = (bf16[32,16,768]{2,1,0:T(8,128)(2,1)S(1)}, bf16[32,16,768]{2,1,0:T(8,128)(2,1)S(1)}, u32[]{:S(2)}, u32[]{:S(2)}) collective-permute-start(bf16[32,16,768]{2,1,0:T(8,128)(2,1)S(1)} %slice.149), channel_id=1, source_target_pairs={{0,96},{32,0},{64,32},{96,64},{1,97},{33,1},{65,33},{97,65},{2,98}... | collective-permute-start | bytes 2359304 | tf_op jit(solution)/shard_map/ppermute | solution.py:395
  162.0 7.8 %collective-permute-start.32 = (bf16[16,64,768]{2,1,0:T(8,128)(2,1)}, bf16[16,64,768]{2,1,0:T(8,128)(2,1)S(1)}, u32[]{:S(2)}, u32[]{:S(2)}) collective-permute-start(bf16[16,64,768]{2,1,0:T(8,128)(2,1)} %get-tuple-element.35), channel_id=1, source_target_pairs={{0,1},{1,0},{2,3},{3,2},{4,5},{5,4},{6,7},{7,6},{8,9},{9,8},{10,11... | collective-permute-start | bytes 4718600 | tf_op jit(solution)/shard_map/ppermute | solution.py:409
  162.5 37.8 %collective-permute-start.40 = (bf16[64,16,768]{2,1,0:T(8,128)(2,1)}, bf16[64,16,768]{2,1,0:T(8,128)(2,1)S(1)}, u32[]{:S(2)}, u32[]{:S(2)}) collective-permute-start(bf16[64,16,768]{2,1,0:T(8,128)(2,1)} %get-tuple-element.38), channel_id=1, source_target_pairs={{0,32},{32,64},{64,96},{96,0},{1,33},{33,65},{65,97},{97,1},{2,34}... | collective-permute-start | bytes 4718600 | tf_op jit(solution)/shard_map/ppermute | solution.py:395
  162.5 37.8 %collective-permute-start.41 = (bf16[64,16,768]{2,1,0:T(8,128)(2,1)}, bf16[64,16,768]{2,1,0:T(8,128)(2,1)S(1)}, u32[]{:S(2)}, u32[]{:S(2)}) collective-permute-start(bf16[64,16,768]{2,1,0:T(8,128)(2,1)} %get-tuple-element.39), channel_id=1, source_target_pairs={{0,96},{32,0},{64,32},{96,64},{1,97},{33,1},{65,33},{97,65},{2,98}... | collective-permute-start | bytes 4718600 | tf_op jit(solution)/shard_map/ppermute | solution.py:395
  167.7 11.1 %collective-permute-start.27 = (bf16[4,64,768]{2,1,0:T(8,128)(2,1)S(1)}, bf16[4,64,768]{2,1,0:T(8,128)(2,1)S(1)}, u32[]{:S(2)}, u32[]{:S(2)}) collective-permute-start(bf16[4,64,768]{2,1,0:T(8,128)(2,1)S(1)} %get-tuple-element.66), channel_id=1, source_target_pairs={{0,24},{1,25},{2,26},{3,27},{4,28},{5,29},{6,30},{7,31},{8,0},{9,1... | collective-permute-start | bytes 1179656 | tf_op jit(solution)/shard_map/ppermute | solution.py:409
  167.8 12.3 %collective-permute-start.25 = (bf16[4,64,768]{2,1,0:T(8,128)(2,1)S(1)}, bf16[4,64,768]{2,1,0:T(8,128)(2,1)S(1)}, u32[]{:S(2)}, u32[]{:S(2)}) collective-permute-start(bf16[4,64,768]{2,1,0:T(8,128)(2,1)S(1)} %get-tuple-element.67), channel_id=1, source_target_pairs={{0,8},{1,9},{2,10},{3,11},{4,12},{5,13},{6,14},{7,15},{8,16},{9,17... | collective-permute-start | bytes 1179656 | tf_op jit(solution)/shard_map/ppermute | solution.py:409
  170.4 10.5 %collective-permute-start.35 = (bf16[4,64,768]{2,1,0:T(8,128)(2,1)S(1)}, bf16[4,64,768]{2,1,0:T(8,128)(2,1)S(1)}, u32[]{:S(2)}, u32[]{:S(2)}) collective-permute-start(bf16[4,64,768]{2,1,0:T(8,128)(2,1)S(1)} %get-tuple-element.70), channel_id=1, source_target_pairs={{0,6},{1,7},{2,0},{3,1},{4,2},{5,3},{6,4},{7,5},{8,14},{9,15},{10,... | collective-permute-start | bytes 1179656 | tf_op jit(solution)/shard_map/ppermute | solution.py:409
  178.8 11.4 %collective-permute-start.33 = (bf16[4,64,768]{2,1,0:T(8,128)(2,1)S(1)}, bf16[4,64,768]{2,1,0:T(8,128)(2,1)S(1)}, u32[]{:S(2)}, u32[]{:S(2)}) collective-permute-start(bf16[4,64,768]{2,1,0:T(8,128)(2,1)S(1)} %get-tuple-element.71), channel_id=1, source_target_pairs={{0,2},{1,3},{2,4},{3,5},{4,6},{5,7},{6,0},{7,1},{8,10},{9,11},{10,... | collective-permute-start | bytes 1179656 | tf_op jit(solution)/shard_map/ppermute | solution.py:409
  180.2 24.8 %collective-permute-start.28 = (bf16[2,64,768]{2,1,0:T(8,128)(2,1)S(1)}, bf16[2,64,768]{2,1,0:T(8,128)(2,1)S(1)}, u32[]{:S(2)}, u32[]{:S(2)}) collective-permute-start(bf16[2,64,768]{2,1,0:T(8,128)(2,1)S(1)} %get-tuple-element.64), channel_id=1, source_target_pairs={{0,24},{1,25},{2,26},{3,27},{4,28},{5,29},{6,30},{7,31},{8,0},{9,1... | collective-permute-start | bytes 589832 | tf_op jit(solution)/shard_map/ppermute | solution.py:409
  180.9 24.2 %collective-permute-start.26 = (bf16[2,64,768]{2,1,0:T(8,128)(2,1)S(1)}, bf16[2,64,768]{2,1,0:T(8,128)(2,1)S(1)}, u32[]{:S(2)}, u32[]{:S(2)}) collective-permute-start(bf16[2,64,768]{2,1,0:T(8,128)(2,1)S(1)} %get-tuple-element.65), channel_id=1, source_target_pairs={{0,8},{1,9},{2,10},{3,11},{4,12},{5,13},{6,14},{7,15},{8,16},{9,17... | collective-permute-start | bytes 589832 | tf_op jit(solution)/shard_map/ppermute | solution.py:409
  190.3 15.7 %collective-permute-start.36 = (bf16[2,64,768]{2,1,0:T(8,128)(2,1)S(1)}, bf16[2,64,768]{2,1,0:T(8,128)(2,1)S(1)}, u32[]{:S(2)}, u32[]{:S(2)}) collective-permute-start(bf16[2,64,768]{2,1,0:T(8,128)(2,1)S(1)} %get-tuple-element.68), channel_id=1, source_target_pairs={{0,6},{1,7},{2,0},{3,1},{4,2},{5,3},{6,4},{7,5},{8,14},{9,15},{10,... | collective-permute-start | bytes 589832 | tf_op jit(solution)/shard_map/ppermute | solution.py:409
  200.3 8.9 %collective-permute-start.34 = (bf16[2,64,768]{2,1,0:T(8,128)(2,1)S(1)}, bf16[2,64,768]{2,1,0:T(8,128)(2,1)S(1)}, u32[]{:S(2)}, u32[]{:S(2)}) collective-permute-start(bf16[2,64,768]{2,1,0:T(8,128)(2,1)S(1)} %get-tuple-element.69), channel_id=1, source_target_pairs={{0,2},{1,3},{2,4},{3,5},{4,6},{5,7},{6,0},{7,1},{8,10},{9,11},{10,... | collective-permute-start | bytes 589832 | tf_op jit(solution)/shard_map/ppermute | solution.py:409
  202.2 26.1 %collective-permute-start.43 = (bf16[32,16,768]{2,1,0:T(8,128)(2,1)S(1)}, bf16[32,16,768]{2,1,0:T(8,128)(2,1)S(1)}, u32[]{:S(2)}, u32[]{:S(2)}) collective-permute-start(bf16[32,16,768]{2,1,0:T(8,128)(2,1)S(1)} %add_convert_fusion.2), channel_id=1, source_target_pairs={{0,96},{32,0},{64,32},{96,64},{1,97},{33,1},{65,33},{97,65},{2,98}... | collective-permute-start | bytes 2359304 | tf_op jit(solution)/shard_map/ppermute | solution.py:395
  205.0 23.5 %collective-permute-start.42 = (bf16[32,16,768]{2,1,0:T(8,128)(2,1)S(1)}, bf16[32,16,768]{2,1,0:T(8,128)(2,1)S(1)}, u32[]{:S(2)}, u32[]{:S(2)}) collective-permute-start(bf16[32,16,768]{2,1,0:T(8,128)(2,1)S(1)} %add_convert_fusion.3), channel_id=1, source_target_pairs={{0,32},{32,64},{64,96},{96,0},{1,33},{33,65},{65,97},{97,1},{2,34}... | collective-permute-start | bytes 2359304 | tf_op jit(solution)/shard_map/ppermute | solution.py:395
  205.9 6.2 %collective-permute-start.29 = (bf16[1,64,768]{2,1,0:T(8,128)(2,1)S(1)}, bf16[1,64,768]{2,1,0:T(8,128)(2,1)S(1)}, u32[]{:S(2)}, u32[]{:S(2)}) collective-permute-start(bf16[1,64,768]{2,1,0:T(8,128)(2,1)S(1)} %get-tuple-element.72), channel_id=1, source_target_pairs={{0,2},{1,3},{2,4},{3,5},{4,6},{5,7},{6,0},{7,1},{8,10},{9,11},{10,... | collective-permute-start | bytes 294920 | tf_op jit(solution)/shard_map/ppermute | solution.py:409
  206.0 6.4 %collective-permute-start.31 = (bf16[1,64,768]{2,1,0:T(8,128)(2,1)S(1)}, bf16[1,64,768]{2,1,0:T(8,128)(2,1)S(1)}, u32[]{:S(2)}, u32[]{:S(2)}) collective-permute-start(bf16[1,64,768]{2,1,0:T(8,128)(2,1)S(1)} %get-tuple-element.73), channel_id=1, source_target_pairs={{0,6},{1,7},{2,0},{3,1},{4,2},{5,3},{6,4},{7,5},{8,14},{9,15},{10,... | collective-permute-start | bytes 294920 | tf_op jit(solution)/shard_map/ppermute | solution.py:409
  209.2 6.1 %collective-permute-start.30 = (bf16[1,64,768]{2,1,0:T(8,128)(2,1)S(1)}, bf16[1,64,768]{2,1,0:T(8,128)(2,1)S(1)}, u32[]{:S(2)}, u32[]{:S(2)}) collective-permute-start(bf16[1,64,768]{2,1,0:T(8,128)(2,1)S(1)} %get-tuple-element.74), channel_id=1, source_target_pairs={{0,4},{1,5},{2,6},{3,7},{4,0},{5,1},{6,2},{7,3},{8,12},{9,13},{10,... | collective-permute-start | bytes 294920 | tf_op jit(solution)/shard_map/ppermute | solution.py:409
  212.1 12.9 %collective-permute-start.37 = (bf16[1,64,768]{2,1,0:T(8,128)(2,1)S(1)}, bf16[1,64,768]{2,1,0:T(8,128)(2,1)S(1)}, u32[]{:S(2)}, u32[]{:S(2)}) collective-permute-start(bf16[1,64,768]{2,1,0:T(8,128)(2,1)S(1)} %get-tuple-element.75), channel_id=1, source_target_pairs={{0,8},{1,9},{2,10},{3,11},{4,12},{5,13},{6,14},{7,15},{8,16},{9,17... | collective-permute-start | bytes 294920 | tf_op jit(solution)/shard_map/ppermute | solution.py:409
  212.4 12.5 %collective-permute-start.39 = (bf16[1,64,768]{2,1,0:T(8,128)(2,1)S(1)}, bf16[1,64,768]{2,1,0:T(8,128)(2,1)S(1)}, u32[]{:S(2)}, u32[]{:S(2)}) collective-permute-start(bf16[1,64,768]{2,1,0:T(8,128)(2,1)S(1)} %get-tuple-element.76), channel_id=1, source_target_pairs={{0,24},{1,25},{2,26},{3,27},{4,28},{5,29},{6,30},{7,31},{8,0},{9,1... | collective-permute-start | bytes 294920 | tf_op jit(solution)/shard_map/ppermute | solution.py:409
  215.3 12.2 %collective-permute-start.38 = (bf16[1,64,768]{2,1,0:T(8,128)(2,1)S(1)}, bf16[1,64,768]{2,1,0:T(8,128)(2,1)S(1)}, u32[]{:S(2)}, u32[]{:S(2)}) collective-permute-start(bf16[1,64,768]{2,1,0:T(8,128)(2,1)S(1)} %get-tuple-element.77), channel_id=1, source_target_pairs={{0,16},{1,17},{2,18},{3,19},{4,20},{5,21},{6,22},{7,23},{8,24},{9,... | collective-permute-start | bytes 294920 | tf_op jit(solution)/shard_map/ppermute | solution.py:409
  (46 other events, 476.8 us)
